TPU v7x, 256 devices: a whole 4x4x8 slice. The times are simulated.
256 devices in a mesh: chan: 8 (over z), tm: 32 (over y, x, core).
Axes of the slice: x: 4, y: 4, z: 8, core: 2. Of those that a mesh axis runs over, the one named last changes fastest.
Arguments:
- symbols: int32 [64, 262144], P('chan', 'tm'), may hold values from 0 to 63
- incidence: int32 [256, 6], P('chan'), may hold values from 0 to 63, as said below
- delays: int32 [256, 6], P('chan'), may hold values from 0 to 63
- gains: float32 [2, 256, 6], P(None, 'chan'), may hold values from -4 to 4
- echoes: bfloat16 [2, 256, 262144], P(None, 'chan', 'tm'), may hold values from -6 to 6
Outputs:
- cancelled: bfloat16 [2, 256, 262144], P(None, 'chan', 'tm')
- weights: float32 [2, 256, 384], P(None, 'chan')
Inputs may be any that keep to these rules, and one draw needn't show every extreme that they name: `incidence`: row r names 6 distinct illuminators, all owned by chan index c = r // 32 or the next index c + 1 taken cyclically: ids from c * 8 to (c + 2) * 8 - 1, modulo 64.
All inputs are finite; a program needn't handle non-finite values.
Results may differ from a plain program's by a relative error of at most 0.024.
Values may be sent and summed in bfloat16 or wider, within the bound.
No kernel may reach another device: no remote copies, remote signals or barrier semaphores. Data moves between devices by JAX's collectives and lax.ppermute only.
A program may use at most 64 MiB of HBM per device.

v0:
```python
import math

import jax
import jax.numpy as jnp
from jax import lax
from jax.sharding import PartitionSpec as P

ACTIVE = 6817
DELAYS = 64
PER_RECV = 6


loading = 0.1
batch_rows = 8
HIGHEST = lax.Precision.HIGHEST


def passed_along(array, axis, by):
    peers = lax.axis_size(axis)
    return lax.ppermute(array, axis, [(i, (i + by) % peers) for i in range(peers)])


def from_behind(block, axis, distance):
    devices = range(lax.axis_size(axis))
    route = [(i - distance, i) for i in devices if i - distance in devices]
    return lax.ppermute(block, axis, route)


def rotation_angle_grid(row_count, col_count, period):
    product = (
        jnp.arange(row_count, dtype=jnp.int32)[:, None]
        * jnp.arange(col_count, dtype=jnp.int32)[None, :]
    )
    phases = (product % period).astype(jnp.float32) * (2.0 * math.pi / period)
    return (jnp.cos(phases), jnp.sin(phases))


def complex_multiply_result(pattern, left_pair, right_pair):
    real_part = jnp.einsum(pattern, left_pair[0], right_pair[0], precision=HIGHEST) - jnp.einsum(
        pattern, left_pair[1], right_pair[1], precision=HIGHEST
    )
    imag_part = jnp.einsum(pattern, left_pair[0], right_pair[1], precision=HIGHEST) + jnp.einsum(
        pattern, left_pair[1], right_pair[0], precision=HIGHEST
    )
    return (real_part, imag_part)


def remodulate(symbols):
    emitter_number, length = symbols.shape
    column_entries = 128
    increment_spacing = length // column_entries
    inphase_amplitude = (2 * (symbols % 8) - 7).astype(jnp.float32) / math.sqrt(42.0)
    quadrature_amplitude = (2 * (symbols // 8) - 7).astype(jnp.float32) / math.sqrt(42.0)
    subcarrier = jnp.arange(length, dtype=jnp.int32) - length // 2
    occupied_tones = (jnp.abs(subcarrier) <= (ACTIVE - 1) // 2).astype(jnp.float32)
    tone_symbols = (
        (inphase_amplitude * occupied_tones).reshape(
            emitter_number, increment_spacing, column_entries
        ),
        (quadrature_amplitude * occupied_tones).reshape(
            emitter_number, increment_spacing, column_entries
        ),
    )
    partial_result = complex_multiply_result(
        "mb,nbd->nmd",
        rotation_angle_grid(increment_spacing, increment_spacing, increment_spacing),
        tone_symbols,
    )
    twiddle = rotation_angle_grid(increment_spacing, column_entries, length)
    partial_result = (
        partial_result[0] * twiddle[0] - partial_result[1] * twiddle[1],
        partial_result[0] * twiddle[1] + partial_result[1] * twiddle[0],
    )
    frequency_spectrum = complex_multiply_result(
        "pho,oj->phj",
        partial_result,
        rotation_angle_grid(column_entries, column_entries, column_entries),
    )
    alternate = (1 - 2 * (jnp.arange(length, dtype=jnp.int32) % 2)).astype(jnp.float32) / math.sqrt(
        ACTIVE
    )
    real_part = (
        jnp.swapaxes(frequency_spectrum[0], 1, 2).reshape(emitter_number, length) * alternate
    )
    imag_part = (
        jnp.swapaxes(frequency_spectrum[1], 1, 2).reshape(emitter_number, length) * alternate
    )
    return jnp.stack([real_part, imag_part], axis=1).astype(jnp.bfloat16)


def lag_table(lag_count):
    spread = jnp.arange(2 * lag_count, dtype=jnp.int32)[:, None, None]
    column = jnp.arange(lag_count, dtype=jnp.int32)[None, :, None]
    lag_pos = jnp.arange(lag_count, dtype=jnp.int32)[None, None, :]
    return (spread == lag_count + column - lag_pos).astype(jnp.float32)


def lag_sums(outer):
    leading = outer.shape[:-2]
    lag_count = outer.shape[-2]
    width = outer.shape[-1]
    flat = outer.reshape(leading + (lag_count * width,))
    flat = jnp.pad(flat, [(0, 0)] * len(leading) + [(0, lag_count)])
    skewed = flat.reshape(leading + (lag_count, width + 1))[..., 1 : lag_count + 1]
    return jnp.flip(jnp.sum(skewed, axis=-2), axis=-1)


def toeplitz_tables(lag_count):
    row_pos = jnp.arange(lag_count, dtype=jnp.int32)[:, None, None]
    col_pos = jnp.arange(lag_count, dtype=jnp.int32)[None, :, None]
    lag_pos = jnp.arange(lag_count, dtype=jnp.int32)[None, None, :]
    lower_part = (row_pos - col_pos == lag_pos).astype(jnp.float32)
    upper_part = ((col_pos - row_pos == lag_pos) & (lag_pos > 0)).astype(jnp.float32)
    return (lower_part, upper_part)


def banded_apply(looked, banded):
    real_part = jnp.einsum(
        "bkqv,bkvp->bqp", looked[:, :, 0], banded[0], preferred_element_type=jnp.float32
    ) - jnp.einsum("bkqv,bkvp->bqp", looked[:, :, 1], banded[1], preferred_element_type=jnp.float32)
    imag_part = jnp.einsum(
        "bkqv,bkvp->bqp", looked[:, :, 0], banded[1], preferred_element_type=jnp.float32
    ) + jnp.einsum("bkqv,bkvp->bqp", looked[:, :, 1], banded[0], preferred_element_type=jnp.float32)
    return (real_part, imag_part)


def local(symbols, incidence, delays, gains, echoes):
    local_refs = remodulate(symbols)
    owned = local_refs.shape[0]
    length = local_refs.shape[2]
    lag_count = DELAYS
    taps_count = PER_RECV * DELAYS
    chan_count = lax.axis_size("chan")
    chan_index = lax.axis_index("chan")
    window_count = 2 * owned
    following = passed_along(local_refs, "chan", -1)
    window = jnp.concatenate([local_refs, following], axis=0)
    previous = from_behind(window[:, :, length - lag_count :], "tm", 1)
    extended = jnp.concatenate([previous, window], axis=2)
    block_count = length // lag_count
    pieces = extended.reshape(window_count, 2, block_count + 1, lag_count)
    frames = jnp.concatenate([pieces[:, :, :-1], pieces[:, :, 1:]], axis=3)
    current = pieces[:, :, 1:]
    tm_count = lax.axis_size("tm")
    tm_index = lax.axis_index("tm")
    scale = 1.0 / (length * tm_count)
    diagonal_table = lag_table(lag_count)
    lag_range = jnp.arange(lag_count, dtype=jnp.int32)

    def pair_row(frame):
        real_part = jnp.einsum(
            "qv,jqp->jpv", frame[0], current[:, 0], preferred_element_type=jnp.float32
        ) + jnp.einsum("qv,jqp->jpv", frame[1], current[:, 1], preferred_element_type=jnp.float32)
        imag_part = jnp.einsum(
            "qv,jqp->jpv", frame[0], current[:, 1], preferred_element_type=jnp.float32
        ) - jnp.einsum("qv,jqp->jpv", frame[1], current[:, 0], preferred_element_type=jnp.float32)
        return jnp.concatenate([lag_sums(real_part), lag_sums(imag_part)], axis=1)

    corr_part = lax.map(pair_row, frames) * scale
    owner_chan = incidence // owned
    slot = (owner_chan - chan_index) % chan_count * owned + incidence % owned
    recv_count = echoes.shape[1]
    group_count = recv_count // batch_rows

    def first_pass(step, carry):
        received_all, cross_all = carry
        start = step * batch_rows
        slots = lax.dynamic_slice_in_dim(slot, start, batch_rows, 0).reshape(-1)
        lag_values = lax.dynamic_slice_in_dim(delays, start, batch_rows, 0)
        gain = lax.dynamic_slice_in_dim(gains, start, batch_rows, 1)
        echo = lax.dynamic_slice_in_dim(echoes, start, batch_rows, 1)
        looked = jnp.take(frames, slots, axis=0).reshape(
            batch_rows, PER_RECV, 2, block_count, 2 * lag_count
        )
        onehot = (lag_values[:, :, None] == lag_range[None, None, :]).astype(jnp.float32)
        gain_taps = gain[:, :, :, None] * onehot[None]
        band = jnp.einsum("vpa,xbka->xbkvp", diagonal_table, gain_taps, precision=HIGHEST)
        band_high = band.astype(jnp.bfloat16)
        band_low = (band - band_high.astype(jnp.float32)).astype(jnp.bfloat16)
        high_re, high_im = banded_apply(looked, band_high)
        low_re, low_im = banded_apply(looked, band_low)
        direct_re = (high_re + low_re).reshape(batch_rows, length)
        direct_im = (high_im + low_im).reshape(batch_rows, length)
        received = jnp.stack(
            [echo[0].astype(jnp.float32) + direct_re, echo[1].astype(jnp.float32) + direct_im]
        ).astype(jnp.bfloat16)
        signal = received.reshape(2, batch_rows, block_count, lag_count)
        real_part = jnp.einsum(
            "bkqv,bqp->bkpv", looked[:, :, 0], signal[0], preferred_element_type=jnp.float32
        ) + jnp.einsum(
            "bkqv,bqp->bkpv", looked[:, :, 1], signal[1], preferred_element_type=jnp.float32
        )
        imag_part = jnp.einsum(
            "bkqv,bqp->bkpv", looked[:, :, 0], signal[1], preferred_element_type=jnp.float32
        ) - jnp.einsum(
            "bkqv,bqp->bkpv", looked[:, :, 1], signal[0], preferred_element_type=jnp.float32
        )
        cross_re = lag_sums(real_part).reshape(batch_rows, taps_count)
        cross_im = lag_sums(imag_part).reshape(batch_rows, taps_count)
        cross_piece = jnp.stack([cross_re, cross_im]) * scale
        received_all = lax.dynamic_update_slice_in_dim(received_all, received, start, 1)
        cross_all = lax.dynamic_update_slice_in_dim(cross_all, cross_piece, start, 1)
        return (received_all, cross_all)

    received_init = jnp.zeros((2, recv_count, length), jnp.bfloat16)
    cross_init = jnp.zeros((2, recv_count, taps_count), jnp.float32)
    received_all, cross_all = lax.fori_loop(0, group_count, first_pass, (received_init, cross_init))
    share = recv_count // tm_count
    corr = lax.psum(corr_part, "tm")
    cross = lax.psum_scatter(cross_all, "tm", scatter_dimension=1, tiled=True)
    mine = lax.dynamic_slice_in_dim(slot, tm_index * share, share, 0)
    selector = (
        mine[:, :, None] == jnp.arange(window_count, dtype=jnp.int32)[None, None, :]
    ).astype(jnp.float32)
    gathered = jnp.einsum("rkw,wvd,rlv->rkld", selector, corr, selector, precision=HIGHEST)
    lower_part, upper_part = toeplitz_tables(lag_count)
    sub_re = gathered[..., :lag_count]
    sub_im = gathered[..., lag_count:]
    gram_re = jnp.einsum("rkld,abd->rkalb", sub_re, lower_part, precision=HIGHEST) + jnp.einsum(
        "rlkd,abd->rkalb", sub_re, upper_part, precision=HIGHEST
    )
    gram_im = jnp.einsum("rkld,abd->rkalb", sub_im, lower_part, precision=HIGHEST) - jnp.einsum(
        "rlkd,abd->rkalb", sub_im, upper_part, precision=HIGHEST
    )
    gram_re = gram_re.reshape(share, taps_count, taps_count) + loading * jnp.eye(
        taps_count, dtype=jnp.float32
    )
    gram_im = gram_im.reshape(share, taps_count, taps_count)
    system = jnp.concatenate(
        [jnp.concatenate([gram_re, -gram_im], axis=2), jnp.concatenate([gram_im, gram_re], axis=2)],
        axis=1,
    )
    factor = jnp.linalg.cholesky(system)
    right_side = jnp.concatenate([cross[0], cross[1]], axis=1)
    solved = jax.vmap(
        lambda chol_factor, vector: jax.scipy.linalg.cho_solve((chol_factor, True), vector)
    )(factor, right_side)
    local_weights = jnp.stack([solved[:, :taps_count], solved[:, taps_count:]])
    weights = lax.all_gather(local_weights, "tm", axis=1, tiled=True)
    taps = weights.astype(jnp.bfloat16).reshape(2, recv_count, PER_RECV, lag_count)
    table_half = diagonal_table.astype(jnp.bfloat16)

    def second_pass(step, cancelled_all):
        start = step * batch_rows
        slots = lax.dynamic_slice_in_dim(slot, start, batch_rows, 0).reshape(-1)
        looked = jnp.take(frames, slots, axis=0).reshape(
            batch_rows, PER_RECV, 2, block_count, 2 * lag_count
        )
        tap_rows = lax.dynamic_slice_in_dim(taps, start, batch_rows, 1)
        banded = jnp.einsum(
            "vpa,xbka->xbkvp", table_half, tap_rows, preferred_element_type=jnp.float32
        ).astype(jnp.bfloat16)
        proj_re, proj_im = banded_apply(looked, banded)
        received = lax.dynamic_slice_in_dim(received_all, start, batch_rows, 1).astype(jnp.float32)
        result = jnp.stack(
            [
                received[0] - proj_re.reshape(batch_rows, length),
                received[1] - proj_im.reshape(batch_rows, length),
            ]
        ).astype(jnp.bfloat16)
        return lax.dynamic_update_slice_in_dim(cancelled_all, result, start, 1)

    cancelled = lax.fori_loop(
        0, group_count, second_pass, jnp.zeros((2, recv_count, length), jnp.bfloat16)
    )
    return (cancelled, weights)


def solution(mesh):
    in_specs = (
        P("chan", "tm"),
        P("chan", None),
        P("chan", None),
        P(None, "chan", None),
        P(None, "chan", "tm"),
    )
    out_specs = (P(None, "chan", "tm"), P(None, "chan", None))
    return jax.shard_map(local, mesh=mesh, in_specs=in_specs, out_specs=out_specs, check_vma=False)
```

profile of v0, /device:TPU:1, one launch (start us, length us, event | category | flops | bytes accessed | tf_op | source)
XLA Modules:
  0.0 829.2 jit_solution(11951167454591355933)
XLA Ops:
  14.2 6.5 collective-permute-start
  34.3 95.9 %while.45 = (s32[]{:T(128)}, f32[16,16,128]{2,0,1:T(8,128)S(1)}, bf16[16,2,128,128]{3,2,1,0:T(8,128)(2,1)S(1)}, bf16[16,2,128,64]{2,3,0,1:T(8,128)(2,1)}, s32[]{:T(128)}, /*index=5*/s32[]{:T(128)}, s32[]{}, f32[]{:T(128)}) while((s32[]{:T(128)}, f32[16,16,128]{2,0,1:T(8,128)S(1)}, bf16[16,2,128,128]{3,2,1,0:T(8,128)(2,1)S(1)}, ...), condition=%wide.region_3.4_spmd, body=%wide.region_0.3_spmd.sunk | while | flops 134610944 | bytes 14368901 | solution.py:159
  132.6 204.2 %while.47 = (s32[]{:T(128)}, bf16[2,32,8192]{2,1,0:T(8,128)(2,1)}, f32[2,32,384]{2,0,1:T(2,128)}, bf16[2,32,8192]{2,1,0:T(8,128)(2,1)}, s32[32,6]{1,0:T(8,128)S(...) while((s32[]{:T(128)}, bf16[2,32,8192]{2,1,0:T(8,128)(2,1)}, ...), condition=%wide.region_20.22_spmd.clone, body=%wide.region_17.21_spmd.clone.sunk | while | flops 1820216704 | bytes 142606928 | solution.py:207
  162.3 5.2 reshape.1090
  213.1 5.2 reshape.1090
  264.0 5.2 reshape.1090
  314.9 5.2 reshape.1090
  337.6 111.2 %all-reduce.9.cloned.1.call-done = (f32[16,16,128]{2,0,1:T(8,128)}, f32[2,32,384]{2,0,1:T(2,128)}) async-done(((f32[16,16,128]{2,0,1:T(8,128)}, f32[2,32,384]{2,0,1:T(2,128)}), (f32[16,16,128]{2,0,1:T(8,128)}, f32[2,32,384]{2,0,1:T(2,128)})) %all-reduce.9.cloned.1.call-update) | async-done | bytes 229392 | tf_op jit(solution)/shard_map/psum | solution.py:209
  465.3 5.4 bitcast_add_fusion.1
  484.1 11.7 %custom-call.56 = f32[1,128,128]{2,1,0:T(8,128)S(1)} custom-call(f32[1,128,128]{2,1,0:T(8,128)S(1)} %cholesky.427), custom_call_target="Cholesky" | custom-call | tf_op jit(solution)/shard_map/jit(cholesky)/cholesky | solution.py:233
  496.6 10.6 %custom-call.57 = f32[1,1,128,128]{2,3,1,0:T(8,128)S(1)} custom-call(f32[1,1,128,128]{3,2,1,0:T(8,128)} %get-tuple-element.625), custom_call_target="InvertDiagBlocksLowerTriangular" | custom-call | tf_op jit(solution)/shard_map/jit(cholesky)/cholesky | solution.py:233
  510.8 12.3 %custom-call.58 = f32[1,128,128]{2,1,0:T(8,128)} custom-call(f32[1,128,128]{2,1,0:T(8,128)S(1)} %cholesky.431), custom_call_target="Cholesky" | custom-call | tf_op jit(solution)/shard_map/jit(cholesky)/cholesky | solution.py:233
  525.3 10.8 %custom-call.59 = f32[1,1,128,128]{2,3,1,0:T(8,128)} custom-call(f32[1,1,128,128]{3,2,1,0:T(8,128)S(1)} %get-tuple-element.622), custom_call_target="InvertDiagBlocksLowerTriangular" | custom-call | tf_op jit(solution)/shard_map/jit(cholesky)/cholesky | solution.py:233
  539.7 12.3 %custom-call.60 = f32[1,128,128]{2,1,0:T(8,128)} custom-call(f32[1,128,128]{2,1,0:T(8,128)S(1)} %cholesky.436), custom_call_target="Cholesky" | custom-call | tf_op jit(solution)/shard_map/jit(cholesky)/cholesky | solution.py:233
  553.6 10.4 %custom-call.61 = f32[1,1,128,128]{2,3,1,0:T(8,128)} custom-call(f32[1,1,128,128]{3,2,1,0:T(8,128)S(1)} %get-tuple-element.619), custom_call_target="InvertDiagBlocksLowerTriangular" | custom-call | tf_op jit(solution)/shard_map/jit(cholesky)/cholesky | solution.py:233
  567.5 12.5 %custom-call.62 = f32[1,128,128]{2,1,0:T(8,128)} custom-call(f32[1,128,128]{2,1,0:T(8,128)S(1)} %cholesky.441), custom_call_target="Cholesky" | custom-call | tf_op jit(solution)/shard_map/jit(cholesky)/cholesky | solution.py:233
  581.6 10.4 %custom-call.63 = f32[1,1,128,128]{2,3,1,0:T(8,128)} custom-call(f32[1,1,128,128]{3,2,1,0:T(8,128)S(1)} %get-tuple-element.616), custom_call_target="InvertDiagBlocksLowerTriangular" | custom-call | tf_op jit(solution)/shard_map/jit(cholesky)/cholesky | solution.py:233
  595.3 12.3 %custom-call.64 = f32[1,128,128]{2,1,0:T(8,128)} custom-call(f32[1,128,128]{2,1,0:T(8,128)S(1)} %cholesky.446), custom_call_target="Cholesky" | custom-call | tf_op jit(solution)/shard_map/jit(cholesky)/cholesky | solution.py:233
  609.3 10.4 %custom-call.65 = f32[1,1,128,128]{2,3,1,0:T(8,128)} custom-call(f32[1,1,128,128]{3,2,1,0:T(8,128)S(1)} %get-tuple-element.613), custom_call_target="InvertDiagBlocksLowerTriangular" | custom-call | tf_op jit(solution)/shard_map/jit(cholesky)/cholesky | solution.py:233
  622.1 12.5 %custom-call.66 = f32[1,128,128]{2,1,0:T(8,128)} custom-call(f32[1,128,128]{2,1,0:T(8,128)S(1)} %fusion.93), custom_call_target="Cholesky" | custom-call | tf_op jit(solution)/shard_map/jit(cholesky)/cholesky | solution.py:233
  641.6 21.0 %while.46 = (s32[]{:T(128)}, f32[1,768,768]{2,1,0:T(8,128)}, s32[6,2]{0,1:T(2,128)S(1)}, f32[6,1,128,128]{3,2,1,0:T(8,128)}, s32[]{:T(128)}) while((s32[]{:T(128)}, f32[1,768,768]{2,1,0:T(8,128)}, s32[6,2]{0,1:T(2,128)S(1)}, f32[6,1,128,128]{3,2,1,0:T(8,128)}, s32[]{:T(128)}) %tuple.166), condition=%wide.while_cond, body=%wide.while_body.sunk | while | flops 2 | bytes 132705 | solution.py:236
  662.6 59.8 %custom-call.67 = f32[1,6,128,128]{2,3,1,0:T(8,128)S(1)} custom-call(f32[1,6,128,128]{3,2,1,0:T(8,128)} %bitcast.868), custom_call_target="InvertDiagBlocksLowerTriangular" | custom-call | tf_op jit(solution)/shard_map/vmap(jit(_cho_solve))/triangular_solve | solution.py:236
  738.1 23.6 %all_gather.3 = f32[2,32,384]{2,0,1:T(2,128)S(1)} all-gather(f32[2,1,384]{2,0,1:T(2,128)S(1)} %pad_maximum_fusion.5), channel_id=1, replica_groups=mesh['chan'=8,'tm'=32] {'tm'}, dimensions={1}, use_global_device_ids=true | all-gather | bytes 101376 | tf_op jit(solution)/shard_map/all_gather | solution.py:239
  764.2 57.8 %while.48 = (s32[]{:T(128)}, bf16[2,32,8192]{2,1,0:T(8,128)(2,1)}, bf16[2,32,8192]{2,1,0:T(8,128)(2,1)}, s32[32,6]{1,0:T(8,128)S(1)}, bf16[16,2,128,128]{3,2,1,0...) while((s32[]{:T(128)}, bf16[2,32,8192]{2,1,0:T(8,128)(2,1)}, ...), condition=%wide.region_23.25_spmd.clone, body=%wide.region_22.24_spmd.clone.sunk | while | flops 508298688 | bytes 64534532 | solution.py:263
  (824 shorter events, 452.2 us)
Async XLA Ops:
  7.2 441.6 %all-reduce.9.cloned.1.call-start = ((), (), s32[]{:S(2)}) async-start(), calls=%async_computation | async-start | bytes 458752 | tf_op jit(solution)/shard_map/psum | solution.py:209
  12.9 8.4 %copy-start.17 = (s32[32,6]{0,1:T(8,128)S(1)}, s32[32,6]{0,1:T(8,128)}, u32[]{:S(2)}) copy-start(s32[32,6]{0,1:T(8,128)} %param.14) | copy-start | bytes 2308
  14.2 11.5 %collective-permute-start = (bf16[8,2,8192]{2,0,1:T(8,128)(2,1)S(1)}, bf16[8,2,8192]{2,0,1:T(8,128)(2,1)S(1)}, u32[]{:S(2)}, u32[]{:S(2)}) collective-permute-start(bf16[8,2,8192]{2,0,1:T(8,128)(2,1)S(1)} %pad_maximum_fusion.2), channel_id=1, source_target_pairs={{0,224},{32,0},{64,32},{96,64},{128,96},{160,128},{192,160},{224,1... | collective-permute-start | bytes 786440 | tf_op jit(solution)/shard_map/ppermute | solution.py:20
  25.7 5.3 collective-permute-start.1
  34.3 98.4 %copy-start.15 = (f32[2,32,6]{1,0,2:T(2,128)S(1)}, f32[2,32,6]{1,0,2:T(2,128)}, u32[]{:S(2)}) copy-start(f32[2,32,6]{1,0,2:T(2,128)} %param.16) | copy-start | bytes 4612
  34.3 98.4 %copy-start.16 = (s32[32,6]{0,1:T(8,128)S(1)}, s32[32,6]{0,1:T(8,128)}, u32[]{:S(2)}) copy-start(s32[32,6]{0,1:T(8,128)} %param.15) | copy-start | bytes 2308
  132.6 204.3 %copy-start.19 = (u32[256]{0:T(256)S(1)}, u32[256]{0:T(256)}, u32[]{:S(2)}) copy-start(u32[256]{0:T(256)} %constant.562) | copy-start | bytes 3076
  132.6 317.6 %copy-start.14 = (s32[64,64]{1,0:T(8,128)S(1)}, s32[64,64]{1,0:T(8,128)}, u32[]{:S(2)}) copy-start(s32[64,64]{1,0:T(8,128)} %iota_subtract_fusion.1) | copy-start | bytes 49156
  138.3 5.5 copy-start.5
  143.8 3.0 copy-start
  147.9 2.6 copy-start.1
  189.2 5.5 copy-start.5
  194.7 3.0 copy-start
  198.8 2.6 copy-start.1
  240.1 5.5 copy-start.5
  245.5 3.0 copy-start
  291.0 5.5 copy-start.5
  296.4 3.0 copy-start
  336.9 120.8 %copy-start.18 = (pred[64]{0:T(512)(128)(4,1)S(1)}, pred[64]{0:T(512)(128)(4,1)}, u32[]{:S(2)}) copy-start(pred[64]{0:T(512)(128)(4,1)} %iota_compare_fusion.11) | copy-start | bytes 196
  464.3 10.7 %copy-start.7 = (f32[1,384,384]{1,2,0:T(8,128)}, f32[1,384,384]{1,2,0:T(8,128)S(1)}, u32[]{:S(2)}) copy-start(f32[1,384,384]{1,2,0:T(8,128)S(1)} %reshape.1060) | copy-start | bytes 1769476
  769.9 2.7 copy-start.3
  784.3 2.7 copy-start.3
  798.7 2.7 copy-start.3
  813.1 2.7 copy-start.3
  (21 other events, 37.5 us)
Sparse Core Ops, SparseCore 0:
  337.0 111.7 all-reduce.8
where the time goes:
time: 838 us; the launch traced here: 829 us
  other arithmetic  266 us (32%)
  local copies, waits for them, and re-layouts  230 us (27%)
  matrix products  160 us (19%)
  waiting for transfers between devices  115 us (14%)
  blocking collectives  23.6 us (3%)
  between operations  18.7 us (2%)
  starting transfers between devices  11.3 us (1%)
    another operation x23, other arithmetic, local(): factor = jnp.linalg.cholesky(system)  136 us
    psum x1, waiting for transfers between devices, local(): corr = lax.psum(corr_part, 'tm')  111 us
    reshape x40, local copies, waits for them, and re-layouts, lag_sums(): flat.reshape(leading + (lag_count, width + 1))[..., 1:lag_count + 1]  81.1 us
    another operation x3, other arithmetic, local(): jax.scipy.linalg.cho_solve((chol_factor, True), vector)  61.9 us
    all_gather x1, blocking collectives, local(): weights = lax.all_gather(local_weights, 'tm', axis=1, tiled=True)  23.6 us
    another operation x21, local copies, waits for them, and re-layouts  23.2 us
    reduce_sum x40, other arithmetic, lag_sums(): return jnp.flip(jnp.sum(skewed, axis=-2), axis=-1)  22 us
    dot_general x12, matrix products, banded_apply(): jnp.einsum('bkqv,bkvp->bqp', looked[:, :, 1], banded[1], preferred_elemen...  21 us
  transfers between devices with their start and end apart: 3, of which 2 were waited for; matrix products, arithmetic and copies ran while one was open for 0% of the time, Pallas kernels for 0%

commit v1 on v0

v1 whole, which is shorter than its diff:
```python
import math

import jax
import jax.numpy as jnp
from jax import lax
from jax.experimental import pallas as pl
from jax.experimental.pallas import tpu as pltpu
from jax.sharding import PartitionSpec as P

ACTIVE = 6817
DELAYS = 64
PER_RECV = 6
LANES = 128
FINE = 16
COARSE = DELAYS // FINE


loading = 0.1
HIGHEST = lax.Precision.HIGHEST


def passed_along(array, axis, by):
    peers = lax.axis_size(axis)
    return lax.ppermute(array, axis, [(i, (i + by) % peers) for i in range(peers)])


def from_behind(block, axis, distance):
    devices = range(lax.axis_size(axis))
    route = [(i - distance, i) for i in devices if i - distance in devices]
    return lax.ppermute(block, axis, route)


def rotation_angle_grid(row_count, col_count, period):
    product = (
        jnp.arange(row_count, dtype=jnp.int32)[:, None]
        * jnp.arange(col_count, dtype=jnp.int32)[None, :]
    )
    phases = (product % period).astype(jnp.float32) * (2.0 * math.pi / period)
    return (jnp.cos(phases), jnp.sin(phases))


def complex_multiply_result(pattern, left_pair, right_pair):
    real_part = jnp.einsum(pattern, left_pair[0], right_pair[0], precision=HIGHEST) - jnp.einsum(
        pattern, left_pair[1], right_pair[1], precision=HIGHEST
    )
    imag_part = jnp.einsum(pattern, left_pair[0], right_pair[1], precision=HIGHEST) + jnp.einsum(
        pattern, left_pair[1], right_pair[0], precision=HIGHEST
    )
    return (real_part, imag_part)


def remodulate(symbols):
    emitter_number, length = symbols.shape
    column_entries = 128
    increment_spacing = length // column_entries
    inphase_amplitude = (2 * (symbols % 8) - 7).astype(jnp.float32) / math.sqrt(42.0)
    quadrature_amplitude = (2 * (symbols // 8) - 7).astype(jnp.float32) / math.sqrt(42.0)
    subcarrier = jnp.arange(length, dtype=jnp.int32) - length // 2
    occupied_tones = (jnp.abs(subcarrier) <= (ACTIVE - 1) // 2).astype(jnp.float32)
    tone_symbols = (
        (inphase_amplitude * occupied_tones).reshape(
            emitter_number, increment_spacing, column_entries
        ),
        (quadrature_amplitude * occupied_tones).reshape(
            emitter_number, increment_spacing, column_entries
        ),
    )
    partial_result = complex_multiply_result(
        "mb,nbd->nmd",
        rotation_angle_grid(increment_spacing, increment_spacing, increment_spacing),
        tone_symbols,
    )
    twiddle = rotation_angle_grid(increment_spacing, column_entries, length)
    partial_result = (
        partial_result[0] * twiddle[0] - partial_result[1] * twiddle[1],
        partial_result[0] * twiddle[1] + partial_result[1] * twiddle[0],
    )
    frequency_spectrum = complex_multiply_result(
        "pho,oj->phj",
        partial_result,
        rotation_angle_grid(column_entries, column_entries, column_entries),
    )
    alternate = (1 - 2 * (jnp.arange(length, dtype=jnp.int32) % 2)).astype(jnp.float32) / math.sqrt(
        ACTIVE
    )
    real_part = (
        jnp.swapaxes(frequency_spectrum[0], 1, 2).reshape(emitter_number, length) * alternate
    )
    imag_part = (
        jnp.swapaxes(frequency_spectrum[1], 1, 2).reshape(emitter_number, length) * alternate
    )
    return jnp.stack([real_part, imag_part], axis=0).astype(jnp.bfloat16)


def iota(shape, axis):
    return lax.broadcasted_iota(jnp.int32, shape, axis)


def build_shifted(ref_ref, shifted_ref):
    rows, width = ref_ref.shape
    piece = 640

    def one_piece(step, _):
        start = pl.multiple_of(step * piece, LANES)
        before = pl.multiple_of(jnp.maximum(start - LANES, 0), LANES)
        first = ref_ref[:, pl.ds(before, LANES)].astype(jnp.float32)
        body = ref_ref[:, pl.ds(start, piece)].astype(jnp.float32)
        source = jnp.concatenate([first, body], axis=1)
        for row in range(rows):
            spread = jnp.broadcast_to(source[row : row + 1, :], (FINE, LANES + piece))
            rolled = pltpu.roll(spread, 0, 1, stride=1, stride_axis=0)
            shifted_ref[row * FINE : (row + 1) * FINE, pl.ds(start, piece)] = rolled[
                :, LANES:
            ].astype(jnp.bfloat16)
        return 0

    lax.fori_loop(0, width // piece, one_piece, 0)


def lay_taps(tap_rows, slot_rows, receivers):
    cols = 32 * FINE
    lane = iota((LANES, cols), 1)
    source = iota((LANES, cols), 0)
    fine = lane & (FINE - 1)
    in_part = (lane >> 7) & 1
    col_slot = ((iota((1, cols), 1) >> 8) << 3) + ((iota((1, cols), 1) >> 4) & 7)
    blocks = []
    for coarse in range(COARSE):
        for out_part in range(2):
            part = in_part ^ out_part
            sign = jnp.where((in_part == 1) & (out_part == 0), -1.0, 1.0)
            spread = jnp.where(source == part * DELAYS + coarse * FINE + fine, sign, 0.0)
            wide = jnp.dot(
                tap_rows, spread.astype(jnp.bfloat16), preferred_element_type=jnp.float32
            )
            total = jnp.zeros((receivers, cols), jnp.float32)
            for k in range(PER_RECV):
                rows = slice(k * receivers, (k + 1) * receivers)
                total = total + jnp.where(
                    slot_rows[rows, 0:1] == col_slot, wide[rows, :], 0.0
                )
            blocks.append(total)
    return jnp.concatenate(blocks, axis=0).astype(jnp.bfloat16)


def coarse_sum(spread):
    rows = spread.shape[0] // COARSE
    total = spread[:rows, LANES:]
    for coarse in range(1, COARSE):
        total = total + pltpu.roll(spread[coarse * rows : (coarse + 1) * rows], coarse * FINE, 1)[:, LANES:]
    return total


def receive_kernel(
    slot_ref, tap_high_ref, tap_low_ref, slot_rows_ref, refs_ref, echo_ref,
    received_ref, cross_ref, corr_ref, shifted, taps_high, taps_low, signal, outer, tidy, picked,
):
    receivers = echo_ref.shape[0] // 2
    length = echo_ref.shape[1]
    width = length + LANES
    rows = 2 * receivers + 32
    build_shifted(refs_ref, shifted)
    taps_high[...] = lay_taps(tap_high_ref[...], slot_rows_ref[...], receivers)
    taps_low[...] = lay_taps(tap_low_ref[...], slot_rows_ref[...], receivers)
    signal[:, 0:LANES] = jnp.zeros((rows, LANES), jnp.bfloat16)
    signal[:, width : width + LANES] = jnp.zeros((rows, LANES), jnp.bfloat16)
    piece = 512

    def direct(step, _):
        start = pl.multiple_of(step * piece, LANES)
        window = shifted[:, pl.ds(start, LANES + piece)]
        spread = jnp.dot(taps_high[...], window, preferred_element_type=jnp.float32) + jnp.dot(
            taps_low[...], window, preferred_element_type=jnp.float32
        )
        echo = echo_ref[:, pl.ds(start, piece)].astype(jnp.float32)
        heard = (echo + coarse_sum(spread)).astype(jnp.bfloat16)
        received_ref[:, pl.ds(start, piece)] = heard
        after = pl.multiple_of(start + LANES, LANES)
        signal[0 : 2 * receivers, pl.ds(after, piece)] = heard
        signal[2 * receivers : rows, pl.ds(after, piece)] = refs_ref[:, pl.ds(after, piece)]
        return 0

    lax.fori_loop(0, length // piece, direct, 0)
    outer[...] = jnp.zeros(outer.shape, jnp.float32)
    span = 640

    def correlate(step, _):
        start = pl.multiple_of(step * span, LANES)
        ahead = signal[:, pl.ds(start, span + LANES)].astype(jnp.float32)
        moved = [ahead[:, :span].astype(jnp.bfloat16)]
        for coarse in range(1, COARSE):
            moved.append(
                pltpu.roll(ahead, span + LANES - coarse * FINE, 1)[:, :span].astype(jnp.bfloat16)
            )
        outer[...] += lax.dot_general(
            jnp.concatenate(moved, axis=0),
            shifted[:, pl.ds(start, span)],
            (((1,), (1,)), ((), ())),
            preferred_element_type=jnp.float32,
        )
        return 0

    lax.fori_loop(0, width // span, correlate, 0)
    scale = 1.0 / 262144.0
    lane = iota((1, LANES), 1)
    half = receivers
    for slot in range(16):
        base = (slot // 8) * 16 + slot % 8
        total = jnp.zeros((receivers + 16, LANES), jnp.float32)
        for coarse in range(COARSE):
            top = coarse * rows

            def part(out_part, in_part):
                col = (base + in_part * 8) * FINE
                tile = slice(col // LANES * LANES, col // LANES * LANES + LANES)
                first = outer[top + out_part * half : top + (out_part + 1) * half, tile]
                low = top + 2 * half
                own = outer[low + 8 * out_part : low + 8 * out_part + 8, tile]
                other = outer[low + 16 + 8 * out_part : low + 24 + 8 * out_part, tile]
                return jnp.concatenate([first, own, other], axis=0)

            offset = (base * FINE) % LANES
            real = part(0, 0) + part(1, 1)
            imag = part(1, 0) - part(0, 1)
            real = pltpu.roll(real, (coarse * FINE - offset) % LANES, 1)
            imag = pltpu.roll(imag, (DELAYS + coarse * FINE - offset) % LANES, 1)
            total = jnp.where(lane >> 4 == coarse, real, total)
            total = jnp.where(lane >> 4 == COARSE + coarse, imag, total)
        total = total * scale
        tidy[slot * receivers : (slot + 1) * receivers, :] = total[:receivers]
        corr_ref[slot * 16 : (slot + 1) * 16, :] = total[receivers:]
    for k in range(PER_RECV):

        def pick(row, _):
            chosen = slot_ref[row, k] * receivers + row
            picked[pl.ds(row, 1), :] = tidy[pl.ds(chosen, 1), :]
            return 0

        lax.fori_loop(0, receivers, pick, 0, unroll=8)
        cross_ref[:, k * LANES : (k + 1) * LANES] = picked[...]


def receive(slot, tap_high, tap_low, slot_rows, refs, echoes):
    rows, length = echoes.shape
    receivers = rows // 2
    width = length + LANES
    smem = pl.BlockSpec(memory_space=pltpu.SMEM)
    vmem = pl.BlockSpec(memory_space=pltpu.VMEM)
    all_rows = rows + 32
    return pl.pallas_call(
        receive_kernel,
        out_shape=(
            jax.ShapeDtypeStruct((rows, length), jnp.bfloat16),
            jax.ShapeDtypeStruct((receivers, PER_RECV * LANES), jnp.float32),
            jax.ShapeDtypeStruct((256, LANES), jnp.float32),
        ),
        in_specs=[smem, vmem, vmem, vmem, vmem, vmem],
        out_specs=(vmem, vmem, vmem),
        scratch_shapes=[
            pltpu.VMEM((32 * FINE, width), jnp.bfloat16),
            pltpu.VMEM((COARSE * rows, 32 * FINE), jnp.bfloat16),
            pltpu.VMEM((COARSE * rows, 32 * FINE), jnp.bfloat16),
            pltpu.VMEM((all_rows, width + LANES), jnp.bfloat16),
            pltpu.VMEM((COARSE * all_rows, 32 * FINE), jnp.float32),
            pltpu.VMEM((16 * receivers, LANES), jnp.float32),
            pltpu.VMEM((receivers, LANES), jnp.float32),
        ],
        compiler_params=pltpu.CompilerParams(vmem_limit_bytes=48 * 2**20),
        name="receive",
    )(slot, tap_high, tap_low, slot_rows, refs, echoes)


def cancel_kernel(tap_ref, slot_rows_ref, refs_ref, received_ref, out_ref, shifted, taps):
    receivers = received_ref.shape[0] // 2
    length = received_ref.shape[1]
    build_shifted(refs_ref, shifted)
    taps[...] = lay_taps(tap_ref[...], slot_rows_ref[...], receivers)
    piece = 512

    def project(step, _):
        start = pl.multiple_of(step * piece, LANES)
        spread = jnp.dot(
            taps[...], shifted[:, pl.ds(start, LANES + piece)], preferred_element_type=jnp.float32
        )
        received = received_ref[:, pl.ds(start, piece)].astype(jnp.float32)
        out_ref[:, pl.ds(start, piece)] = (received - coarse_sum(spread)).astype(jnp.bfloat16)
        return 0

    lax.fori_loop(0, length // piece, project, 0)


def cancel(taps, slot_rows, refs, received):
    rows, length = received.shape
    vmem = pl.BlockSpec(memory_space=pltpu.VMEM)
    return pl.pallas_call(
        cancel_kernel,
        out_shape=jax.ShapeDtypeStruct((rows, length), jnp.bfloat16),
        in_specs=[vmem] * 4,
        out_specs=vmem,
        scratch_shapes=[
            pltpu.VMEM((32 * FINE, length + LANES), jnp.bfloat16),
            pltpu.VMEM((COARSE * rows, 32 * FINE), jnp.bfloat16),
        ],
        compiler_params=pltpu.CompilerParams(vmem_limit_bytes=40 * 2**20),
        name="cancel",
    )(taps, slot_rows, refs, received)


def times_i(packed):
    sign = jnp.where(iota((1, LANES), 1) < DELAYS, -1.0, 1.0)
    count = packed.shape[1] // LANES
    blocks = [
        pltpu.roll(packed[:, b * LANES : (b + 1) * LANES], DELAYS, 1) * sign for b in range(count)
    ]
    return blocks[0] if count == 1 else jnp.concatenate(blocks, axis=1)


def inverse(block):
    size = block.shape[0]
    lane = iota((1, LANES), 1)
    sub = iota((size, 1), 0)
    sign = jnp.where(lane < DELAYS, -1.0, 1.0)

    def spread(column):
        return jnp.broadcast_to(column, (size, LANES))

    col_re = spread(block[:, 0:1])
    col_im = spread(block[:, DELAYS : DELAYS + 1])
    for p in range(size):
        last = p + 1 == size
        if not last:
            next_re = spread(block[:, p + 1 : p + 2])
            next_im = spread(block[:, DELAYS + p + 1 : DELAYS + p + 2])
        row = block[p : p + 1, :]
        over = 1.0 / col_re[p : p + 1, :]
        row = jnp.where(lane == p, 1.0, jnp.where(lane == DELAYS + p, 0.0, row))
        turned = pltpu.roll(row, DELAYS, 1) * sign
        row = row * over
        turned = turned * over
        if not last:
            fac_re = col_re[p + 1 : p + 2, :] * over
            fac_im = -col_im[p + 1 : p + 2, :] * over
            next_re = next_re - col_re * fac_re + col_im * fac_im
            next_im = next_im - col_re * fac_im - col_im * fac_re
            next_re = jnp.where(sub == p, fac_re, next_re)
            next_im = jnp.where(sub == p, fac_im, next_im)
        block = jnp.where((lane & (DELAYS - 1)) == p, 0.0, block)
        block = block - col_re * row - col_im * turned
        block = jnp.where(sub == p, row, block)
        if not last:
            col_re, col_im = next_re, next_im
    return block


def exact_dot(left, right):
    return jnp.dot(left, right, precision=HIGHEST, preferred_element_type=jnp.float32)


def solve_kernel(slot_ref, corr_ref, cross_ref, out_ref, system, pairs):
    count = PER_RECV
    size = DELAYS
    for k in range(count):
        for l in range(count):
            row = k * count + l
            ahead = slot_ref[k] * 16 + slot_ref[l]
            behind = slot_ref[l] * 16 + slot_ref[k]
            pairs[row : row + 1, 0:LANES] = corr_ref[pl.ds(ahead, 1), :]
            pairs[row : row + 1, LANES : 2 * LANES] = corr_ref[pl.ds(behind, 1), :]
    pairs[count * count :, :] = jnp.zeros((pairs.shape[0] - count * count, 2 * LANES), jnp.float32)
    src = iota((2 * LANES, 2 * LANES), 0)
    dst = iota((2 * LANES, 2 * LANES), 1)
    x = dst & (LANES - 1)
    imag = dst >> 7
    from_ahead = jnp.where(x > size, imag * size + LANES - x, jnp.where(x == 0, imag * size, -1))
    from_behind_lag = jnp.where((x > 0) & (x < size), LANES + imag * size + x, -1)
    order = jnp.where(src == from_ahead, 1.0, 0.0) + jnp.where(
        src == from_behind_lag, jnp.where(imag == 1, -1.0, 1.0), 0.0
    )
    circular = exact_dot(pairs[...], order)
    lane = iota((1, LANES), 1)
    sub = iota((size, 1), 0)
    for k in range(count):
        for l in range(count):
            row = k * count + l
            real = jnp.broadcast_to(circular[row : row + 1, 0:LANES], (size, LANES))
            imag_part = jnp.broadcast_to(circular[row : row + 1, LANES:], (size, LANES))
            real = pltpu.roll(real, 0, 1, stride=1, stride_axis=0)
            imag_part = pltpu.roll(imag_part, size, 1, stride=1, stride_axis=0)
            block = jnp.where(lane < size, real, imag_part)
            if k == l:
                block = block + jnp.where(lane == sub, loading, 0.0)
            system[k * size : (k + 1) * size, l * LANES : (l + 1) * LANES] = block
    lane_sq = iota((LANES, LANES), 1)
    sub_sq = iota((LANES, LANES), 0)
    gather = jnp.where(lane_sq == (sub_sq >> 6) * size, 1.0, 0.0)
    on_diag = (lane & (size - 1)) == sub
    for k in range(count):
        spread = jnp.where(on_diag, cross_ref[:, k * LANES : (k + 1) * LANES], 0.0)
        system[k * size : (k + 1) * size, count * LANES :] = exact_dot(spread, gather)
    for i in range(count):
        mine = slice(i * size, (i + 1) * size)
        col = slice(i * LANES, (i + 1) * LANES)
        rest = slice((i + 1) * LANES, (count + 1) * LANES)
        over = inverse(system[mine, col])
        right = system[mine, rest]
        scaled = exact_dot(over, jnp.concatenate([right, times_i(right)], axis=0))
        both = jnp.concatenate([scaled, times_i(scaled)], axis=0)
        system[:, rest] = system[:, rest] - exact_dot(system[:, col], both)
        system[mine, rest] = scaled
    scatter = jnp.where(sub_sq == (lane_sq >> 6) * size, 1.0, 0.0)
    ones = jnp.ones((8, size), jnp.float32)
    for k in range(count):
        found = exact_dot(system[k * size : (k + 1) * size, count * LANES :], scatter)
        row = exact_dot(ones, jnp.where(on_diag, found, 0.0))
        out_ref[:, k * LANES : (k + 1) * LANES] = row[0:1]


def solve(slot, corr, cross):
    smem = pl.BlockSpec(memory_space=pltpu.SMEM)
    vmem = pl.BlockSpec(memory_space=pltpu.VMEM)
    size = PER_RECV * DELAYS
    return pl.pallas_call(
        solve_kernel,
        out_shape=jax.ShapeDtypeStruct((1, PER_RECV * LANES), jnp.float32),
        in_specs=[smem, vmem, vmem],
        out_specs=vmem,
        scratch_shapes=[
            pltpu.VMEM((size, (PER_RECV + 1) * LANES), jnp.float32),
            pltpu.VMEM((40, 2 * LANES), jnp.float32),
        ],
        name="solve",
    )(slot, corr, cross)


def local(symbols, incidence, delays, gains, echoes):
    owned, length = symbols.shape
    chan_count = lax.axis_size("chan")
    chan_index = lax.axis_index("chan")
    tm_count = lax.axis_size("tm")
    tm_index = lax.axis_index("tm")
    recv_count = echoes.shape[1]
    own = remodulate(symbols).reshape(2 * owned, length)
    following = passed_along(own, "chan", -1)
    window = jnp.concatenate([own, following], axis=0)
    previous = from_behind(window[:, length - LANES :], "tm", 1)
    refs = jnp.concatenate([previous, window], axis=1)
    owner_chan = incidence // owned
    slot = (owner_chan - chan_index) % chan_count * owned + incidence % owned
    slot_rows = jnp.broadcast_to(
        slot.T.reshape(PER_RECV * recv_count, 1), (PER_RECV * recv_count, LANES)
    )
    lag = jnp.arange(LANES, dtype=jnp.int32)
    gain_rows = jnp.where(
        lag < DELAYS,
        gains[0].T.reshape(PER_RECV * recv_count, 1),
        gains[1].T.reshape(PER_RECV * recv_count, 1),
    )
    gain_taps = jnp.where(
        delays.T.reshape(PER_RECV * recv_count, 1) == (lag & (DELAYS - 1)), gain_rows, 0.0
    )
    tap_high = lax.reduce_precision(gain_taps, 8, 7)
    tap_low = (gain_taps - tap_high).astype(jnp.bfloat16)
    received, cross, corr = receive(
        slot, tap_high.astype(jnp.bfloat16), tap_low, slot_rows, refs, echoes.reshape(2 * recv_count, length)
    )
    share = recv_count // tm_count
    corr_share = corr.size // tm_count
    parts = jnp.concatenate([cross, corr.reshape(tm_count, corr_share)], axis=1)
    parts = jnp.sum(lax.all_to_all(parts, "tm", 0, 0, tiled=True), axis=0, keepdims=True)
    my_cross = parts[:, : PER_RECV * LANES]
    my_corr = jnp.broadcast_to(parts[:, PER_RECV * LANES :], (tm_count, corr_share))
    corr = lax.all_to_all(my_corr, "tm", 0, 0, tiled=True).reshape(256, LANES)
    my_slot = lax.dynamic_slice_in_dim(slot, tm_index * share, share, 0).reshape(PER_RECV)
    mine = solve(my_slot, corr, my_cross)
    solved = lax.all_to_all(
        jnp.broadcast_to(mine, (tm_count, PER_RECV * LANES)), "tm", 0, 0, tiled=True
    ).reshape(recv_count, PER_RECV, 2, DELAYS)
    weights = jnp.transpose(solved, (2, 0, 1, 3)).reshape(2, recv_count, PER_RECV * DELAYS)
    taps = jnp.transpose(solved.astype(jnp.bfloat16), (1, 0, 2, 3)).reshape(
        PER_RECV * recv_count, LANES
    )
    cancelled = cancel(taps, slot_rows, refs, received).reshape(2, recv_count, length)
    return (cancelled, weights)


def solution(mesh):
    in_specs = (
        P("chan", "tm"),
        P("chan", None),
        P("chan", None),
        P(None, "chan", None),
        P(None, "chan", "tm"),
    )
    out_specs = (P(None, "chan", "tm"), P(None, "chan", None))
    return jax.shard_map(local, mesh=mesh, in_specs=in_specs, out_specs=out_specs, check_vma=False)
```

time: 838 us -> 146 us (0.17)
  other arithmetic: 266 us -> 2.9 us
  local copies, waits for them, and re-layouts: 230 us -> 5.27 us
  matrix products: 160 us -> 4.62 us
  waiting for transfers between devices: 115 us -> 11.3 us
  Pallas kernels: 0 us -> 77.8 us
  between operations: 18.7 us -> 0.95 us
    another operation x33 -> x1, other arithmetic: 198 us -> 0.04 us  [the longest x23 136 us: local(): factor = jnp.linalg.cholesky(system)]
    dot_general x78 -> x0, matrix products: 114 us -> none  [the longest x12 21 us: banded_apply(): jnp.einsum('bkqv,bkvp->bqp', looked[:, :, 1], banded[1], preferred_elemen...]
    psum x1 -> x0, waiting for transfers between devices: 111 us -> none  [local(): corr = lax.psum(corr_part, 'tm')]
    reshape x86 -> x5, local copies, waits for them, and re-layouts: 103 us -> 1.63 us  [the longest x1 0.74 us: local(): jnp.transpose(solved, (2, 0, 1, 3))]
    pallas_call x0 -> x3, Pallas kernels: none -> 77.8 us  [the longest x1 41.2 us: solve(): pl.pallas_call(solve_kernel, out_shape=jax.ShapeDtypeStruct((1, PER_RECV...]
    all_to_all x0 -> x2, blocking collectives: none -> 27.7 us  [the longest x1 16.6 us: local(): lax.all_to_all(parts, 'tm', 0, 0, tiled=True)]
    another operation x32 -> x0, matrix products: 27.6 us -> none  [the longest x22 14.2 us: local(): jax.scipy.linalg.cho_solve((chol_factor, True), vector)]
    all_gather x1 -> x0, blocking collectives: 23.6 us -> none  [local(): weights = lax.all_gather(local_weights, 'tm', axis=1, tiled=True)]
  transfers between devices with their start and end apart: 3 -> 3, of which waited for: 2 -> 3; matrix products, arithmetic and copies ran while one was open for 0% -> 1% of each run, Pallas kernels for 0% -> 0%
where the time goes in v1:
time: 146 us; the launch traced here: 145 us
  Pallas kernels  77.8 us (53%)
  blocking collectives  27.7 us (19%)
  starting transfers between devices  14.9 us (10%)
  waiting for transfers between devices  11.3 us (8%)
  local copies, waits for them, and re-layouts  5.27 us (4%)
  matrix products  4.62 us (3%)
  other arithmetic  2.9 us (2%)
    pallas_call x1, Pallas kernels, solve(): pl.pallas_call(solve_kernel, out_shape=jax.ShapeDtypeStruct((1, PER_RECV...  41.2 us
    pallas_call x1, Pallas kernels, receive(): pl.pallas_call(receive_kernel, out_shape=(jax.ShapeDtypeStruct((rows, len...  24.1 us
    all_to_all x1, blocking collectives, local(): lax.all_to_all(parts, 'tm', 0, 0, tiled=True)  16.6 us
    pallas_call x1, Pallas kernels, cancel(): pl.pallas_call(cancel_kernel, out_shape=jax.ShapeDtypeStruct((rows, lengt...  12.5 us
    all_to_all x1, blocking collectives, local(): lax.all_to_all(jnp.broadcast_to(mine, (tm_count, PER_RECV * LANES)), 'tm'...  11 us
    ppermute x1, starting transfers between devices, passed_along(): lax.ppermute(array, axis, [(i, (i + by) % peers) for i in range(peers)])  6.46 us
    all_to_all x1, waiting for transfers between devices, local(): corr = lax.all_to_all(my_corr, 'tm', 0, 0, tiled=True).reshape(256, LANES)  6.25 us
    ppermute x1, starting transfers between devices, from_behind(): return lax.ppermute(block, axis, route)  4.51 us
  transfers between devices with their start and end apart: 3, of which 3 were waited for; matrix products, arithmetic and copies ran while one was open for 1% of the time, Pallas kernels for 0%

profile of v1, /device:TPU:1, one launch (start us, length us, event | category | flops | bytes accessed | tf_op | source)
XLA Modules:
  0.0 145.4 jit_solution(14425298765180024726)
XLA Ops:
  0.8 1.2 fusion.8
  2.6 0.5 fusion.15
  3.7 0.5 fusion.2
  4.3 0.6 fusion.26
  4.9 0.6 fusion.30
  5.5 0.6 fusion
  6.5 0.6 fusion.1
  7.7 6.5 %collective-permute-start = (bf16[16,8192]{1,0:T(8,128)(2,1)S(1)}, bf16[16,8192]{1,0:T(8,128)(2,1)S(1)}, u32[]{:S(2)}, u32[]{:S(2)}) collective-permute-start(bf16[16,8192]{1,0:T(8,128)(2,1)S(1)} %maximum_bitcast_fusion), channel_id=1, source_target_pairs={{0,224},{32,0},{64,32},{96,64},{128,96},{160,128},{192,160},{224,1... | collective-permute-start | bytes 786440 | tf_op jit(solution)/shard_map/ppermute | solution.py:24
  14.7 4.4 %collective-permute-done = bf16[16,8192]{1,0:T(8,128)(2,1)S(1)} collective-permute-done((bf16[16,8192]{1,0:T(8,128)(2,1)S(1)}, bf16[16,8192]{1,0:T(8,128)(2,1)S(1)}, u32[]{:S(2)}, u32[]{:S(2)}) %collective-permute-start) | collective-permute-done | bytes 262176 | tf_op jit(solution)/shard_map/ppermute | solution.py:24
  19.1 4.5 %collective-permute-start.1 = (bf16[32,128]{1,0:T(8,128)(2,1)S(1)}, bf16[32,128]{1,0:T(8,128)(2,1)S(1)}, u32[]{:S(2)}, u32[]{:S(2)}) collective-permute-start(bf16[32,128]{1,0:T(8,128)(2,1)S(1)} %pad_maximum_fusion.1), channel_id=1, source_target_pairs={{0,1},{1,2},{2,3},{3,4},{4,5},{5,6},{6,7},{7,8},{8,9},{9,10},{10,1... | collective-permute-start | bytes 24584 | tf_op jit(solution)/shard_map/ppermute | solution.py:30
  23.8 0.6 collective-permute-done.1
  24.5 24.1 %receive.1 = (bf16[64,8192]{1,0:T(8,128)(2,1)S(1)}, f32[32,768]{1,0:T(8,128)S(1)}, f32[256,128]{1,0:T(8,128)S(1)}) custom-call(s32[32,6]{1,0:T(8,128)S(1)} %fusion.68.slot_ref, bf16[192,128]{1,0:T(8,128)(2,1)S(1)} %get-tuple-element.15.tap_high_ref, bf16[192,128]{1,0:T(8,128)(2,1)S(1)} %get-tuple-element.14.tap_low_ref, ...), custom_call_target="tpu_custom_call" | custom-call | tf_op jit(solution)/shard_map/receive/pallas_call | solution.py:250
  48.9 16.6 %all_to_all.21 = f32[32,1,1792]{2,1,0:T(1,128)S(1)} all-to-all(f32[32,1,1792]{2,1,0:T(1,128)S(1)} %all_to_all.14), channel_id=1, replica_groups=mesh['chan'=8,'tm'=32] {'tm'}, dimensions={0} | all-to-all | bytes 458752 | tf_op jit(solution)/shard_map/all_to_all | solution.py:469
  65.7 0.7 broadcast_in_dim.72
  66.4 4.0 %all-to-all-start.1 = ((f32[32,1,1024]{2,1,0:T(1,128)}), f32[32,1,1024]{2,1,0:T(1,128)S(1)}, u32[]{:S(2)}, u32[]{:S(2)}) async-start(f32[32,1,1024]{2,1,0:T(1,128)} %broadcast_in_dim.72), calls=%async_computation.1 | async-start | bytes 262144 | tf_op jit(solution)/shard_map/all_to_all | solution.py:472
  70.3 0.6 dynamic-slice_bitcast_fusion.slot_ref
  70.9 0.6 slice.24.cross_ref
  71.5 6.2 %all-to-all-done.1 = f32[32,1,1024]{2,1,0:T(1,128)S(1)} async-done(((f32[32,1,1024]{2,1,0:T(1,128)}), f32[32,1,1024]{2,1,0:T(1,128)S(1)}, u32[]{:S(2)}, u32[]{:S(2)}) %all-to-all-start.1) | async-done | bytes 131104 | tf_op jit(solution)/shard_map/all_to_all | solution.py:472
  77.8 0.7 copy-done.1
  78.4 41.2 %solve.1 = f32[1,768]{1,0:T(1,128)} custom-call(s32[6]{0:T(128)} %dynamic-slice_bitcast_fusion.slot_ref, f32[256,128]{1,0:T(8,128)} %bitcast.57, f32[1,768]{1,0:T(1,128)} %slice.24.cross_ref), custom_call_target="tpu_custom_call" | custom-call | tf_op jit(solution)/shard_map/solve/pallas_call | solution.py:422
  119.6 0.7 reduce.1
  120.4 11.0 %all_to_all.22 = f32[32,1,768]{2,1,0:T(1,128)S(1)} all-to-all(f32[32,1,768]{2,1,0:T(1,128)S(1)} %broadcast_in_dim.73), channel_id=1, replica_groups=mesh['chan'=8,'tm'=32] {'tm'}, dimensions={0} | all-to-all | bytes 196608 | tf_op jit(solution)/shard_map/all_to_all | solution.py:475
  132.1 0.7 reshape.200
  132.9 12.5 %cancel.1 = bf16[64,8192]{1,0:T(8,128)(2,1)} custom-call(bf16[192,128]{1,0:T(8,128)(2,1)S(1)} %reshape.198.tap_ref, s32[192,128]{1,0:T(8,128)S(1)} %broadcast_in_dim.70.slot_rows_ref, bf16[32,8320]{1,0:T(8,128)(2,1)S(1)} %maximum_maximum_fusion.refs_ref, bf16[64,8192]{1,0:T(8,128)(2,1)S(1)} %get-tuple-element.7.received_ref), custom_call_target="tpu_custom_call" | custom-call | tf_op jit(solution)/shard_map/cancel/pallas_call | solution.py:295
  (49 shorter events, 4.0 us)
Async XLA Ops:
  7.3 6.8 %copy-start.2 = (f32[2,32,6]{1,0,2:T(2,128)S(1)}, f32[2,32,6]{1,0,2:T(2,128)}, u32[]{:S(2)}) copy-start(f32[2,32,6]{1,0,2:T(2,128)} %param.8) | copy-start | bytes 4612
  7.4 6.8 %copy-start.3 = (s32[32,6]{0,1:T(8,128)S(1)}, s32[32,6]{0,1:T(8,128)}, u32[]{:S(2)}) copy-start(s32[32,6]{0,1:T(8,128)} %param.6) | copy-start | bytes 2308
  7.4 6.9 %copy-start.4 = (s32[32,6]{0,1:T(8,128)S(1)}, s32[32,6]{0,1:T(8,128)}, u32[]{:S(2)}) copy-start(s32[32,6]{0,1:T(8,128)} %param.7) | copy-start | bytes 2308
  7.6 16.9 %copy-start = (bf16[2,32,8192]{2,1,0:T(8,128)(2,1)S(1)}, bf16[2,32,8192]{2,1,0:T(8,128)(2,1)}, u32[]{:S(2)}) copy-start(bf16[2,32,8192]{2,1,0:T(8,128)(2,1)} %param.9) | copy-start | bytes 3145732
  7.7 11.5 %collective-permute-start = (bf16[16,8192]{1,0:T(8,128)(2,1)S(1)}, bf16[16,8192]{1,0:T(8,128)(2,1)S(1)}, u32[]{:S(2)}, u32[]{:S(2)}) collective-permute-start(bf16[16,8192]{1,0:T(8,128)(2,1)S(1)} %maximum_bitcast_fusion), channel_id=1, source_target_pairs={{0,224},{32,0},{64,32},{96,64},{128,96},{160,128},{192,160},{224,1... | collective-permute-start | bytes 786440 | tf_op jit(solution)/shard_map/ppermute | solution.py:24
  19.1 5.3 %collective-permute-start.1 = (bf16[32,128]{1,0:T(8,128)(2,1)S(1)}, bf16[32,128]{1,0:T(8,128)(2,1)S(1)}, u32[]{:S(2)}, u32[]{:S(2)}) collective-permute-start(bf16[32,128]{1,0:T(8,128)(2,1)S(1)} %pad_maximum_fusion.1), channel_id=1, source_target_pairs={{0,1},{1,2},{2,3},{3,4},{4,5},{5,6},{6,7},{7,8},{8,9},{9,10},{10,1... | collective-permute-start | bytes 24584 | tf_op jit(solution)/shard_map/ppermute | solution.py:30
  66.4 11.4 %all-to-all-start.1 = ((f32[32,1,1024]{2,1,0:T(1,128)}), f32[32,1,1024]{2,1,0:T(1,128)S(1)}, u32[]{:S(2)}, u32[]{:S(2)}) async-start(f32[32,1,1024]{2,1,0:T(1,128)} %broadcast_in_dim.72), calls=%async_computation.1 | async-start | bytes 262144 | tf_op jit(solution)/shard_map/all_to_all | solution.py:472
  77.8 0.7 copy-start.1

commit v2 on v1

--- a/solution.py
+++ b/solution.py
@@ -13,6 +13,10 @@
 LANES = 128
 FINE = 16
 COARSE = DELAYS // FINE
+PANEL = 4
+SPAN = 640
+PIECE = 1024
+RECEIVE_VMEM = 56 * 2**20
 
 
 loading = 0.1
@@ -96,9 +100,14 @@
     return lax.broadcasted_iota(jnp.int32, shape, axis)
 
 
-def build_shifted(ref_ref, shifted_ref):
+def copy_of(source, target, sems, step, start, size):
+    cols = pl.ds(pl.multiple_of(start, LANES), size)
+    return pltpu.make_async_copy(source.at[:, cols], target.at[:, cols], sems.at[step])
+
+
+def build_shifted(ref_ref, shifted_ref, kept_ref, sems):
     rows, width = ref_ref.shape
-    piece = 640
+    piece = SPAN
 
     def one_piece(step, _):
         start = pl.multiple_of(step * piece, LANES)
@@ -112,6 +121,7 @@
             shifted_ref[row * FINE : (row + 1) * FINE, pl.ds(start, piece)] = rolled[
                 :, LANES:
             ].astype(jnp.bfloat16)
+        copy_of(shifted_ref, kept_ref, sems, step, start, piece).start()
         return 0
 
     lax.fori_loop(0, width // piece, one_piece, 0)
@@ -151,93 +161,140 @@
     return total
 
 
+def moved_ahead(ahead, span):
+    moved = [ahead[:, :span].astype(jnp.bfloat16)]
+    for coarse in range(1, COARSE):
+        moved.append(
+            pltpu.roll(ahead, span + LANES - coarse * FINE, 1)[:, :span].astype(jnp.bfloat16)
+        )
+    return jnp.concatenate(moved, axis=0)
+
+
+def by_lag(read, rows, store):
+    lane = iota((1, LANES), 1)
+    for block in range(2):
+
+        def one_slot(j, _, block=block):
+            total = jnp.zeros((rows, LANES), jnp.float32)
+            for coarse in range(COARSE):
+                real = read(coarse, 0, 2 * block) + read(coarse, 1, 2 * block + 1)
+                imag = read(coarse, 1, 2 * block) - read(coarse, 0, 2 * block + 1)
+                place = coarse * FINE + LANES - j * FINE
+                real = pltpu.roll(real, place, 1)
+                imag = pltpu.roll(imag, place + DELAYS, 1)
+                total = jnp.where(lane >> 4 == coarse, real, total)
+                total = jnp.where(lane >> 4 == COARSE + coarse, imag, total)
+            store(block * 8 + j, total * (1.0 / 262144.0))
+            return 0
+
+        lax.fori_loop(0, 8, one_slot, 0)
+
+
+def fetch_all(kept_ref, shifted, sems, step_size):
+    width = kept_ref.shape[1]
+    lead = width % step_size
+    steps = width // step_size
+    if lead:
+        copy_of(kept_ref, shifted, sems, steps, 0, lead).start()
+    for step in range(steps):
+        copy_of(kept_ref, shifted, sems, step, lead + step * step_size, step_size).start()
+    if lead:
+        copy_of(kept_ref, shifted, sems, steps, 0, lead).wait()
+
+    def arrive(step):
+        copy_of(kept_ref, shifted, sems, step, lead + step * step_size, step_size).wait()
+
+    return arrive
+
+
 def receive_kernel(
     slot_ref, tap_high_ref, tap_low_ref, slot_rows_ref, refs_ref, echo_ref,
-    received_ref, cross_ref, corr_ref, shifted, taps_high, taps_low, signal, outer, tidy, picked,
+    received_ref, cross_ref, corr_ref, kept_ref,
+    shifted, taps_high, taps_low, signal, outer, flipped, tidy, picked, sems,
 ):
     receivers = echo_ref.shape[0] // 2
     length = echo_ref.shape[1]
     width = length + LANES
-    rows = 2 * receivers + 32
-    build_shifted(refs_ref, shifted)
+    heard_rows = 2 * receivers
+    rows = heard_rows + 32
+    build_shifted(refs_ref, shifted, kept_ref, sems)
     taps_high[...] = lay_taps(tap_high_ref[...], slot_rows_ref[...], receivers)
     taps_low[...] = lay_taps(tap_low_ref[...], slot_rows_ref[...], receivers)
     signal[:, 0:LANES] = jnp.zeros((rows, LANES), jnp.bfloat16)
+    signal[heard_rows:rows, LANES:width] = refs_ref[:, LANES:width]
     signal[:, width : width + LANES] = jnp.zeros((rows, LANES), jnp.bfloat16)
-    piece = 512
 
     def direct(step, _):
-        start = pl.multiple_of(step * piece, LANES)
-        window = shifted[:, pl.ds(start, LANES + piece)]
+        start = pl.multiple_of(step * PIECE, LANES)
+        window = shifted[:, pl.ds(start, LANES + PIECE)]
         spread = jnp.dot(taps_high[...], window, preferred_element_type=jnp.float32) + jnp.dot(
             taps_low[...], window, preferred_element_type=jnp.float32
         )
-        echo = echo_ref[:, pl.ds(start, piece)].astype(jnp.float32)
+        echo = echo_ref[:, pl.ds(start, PIECE)].astype(jnp.float32)
         heard = (echo + coarse_sum(spread)).astype(jnp.bfloat16)
-        received_ref[:, pl.ds(start, piece)] = heard
-        after = pl.multiple_of(start + LANES, LANES)
-        signal[0 : 2 * receivers, pl.ds(after, piece)] = heard
-        signal[2 * receivers : rows, pl.ds(after, piece)] = refs_ref[:, pl.ds(after, piece)]
-        return 0
-
-    lax.fori_loop(0, length // piece, direct, 0)
+        received_ref[:, pl.ds(start, PIECE)] = heard
+        signal[0:heard_rows, pl.ds(pl.multiple_of(start + LANES, LANES), PIECE)] = heard
+        return 0
+
+    lax.fori_loop(0, length // PIECE, direct, 0)
     outer[...] = jnp.zeros(outer.shape, jnp.float32)
-    span = 640
 
     def correlate(step, _):
-        start = pl.multiple_of(step * span, LANES)
-        ahead = signal[:, pl.ds(start, span + LANES)].astype(jnp.float32)
-        moved = [ahead[:, :span].astype(jnp.bfloat16)]
-        for coarse in range(1, COARSE):
-            moved.append(
-                pltpu.roll(ahead, span + LANES - coarse * FINE, 1)[:, :span].astype(jnp.bfloat16)
-            )
+        start = pl.multiple_of(step * SPAN, LANES)
         outer[...] += lax.dot_general(
-            jnp.concatenate(moved, axis=0),
-            shifted[:, pl.ds(start, span)],
+            shifted[:, pl.ds(start, SPAN)],
+            moved_ahead(signal[:, pl.ds(start, SPAN + LANES)].astype(jnp.float32), SPAN),
             (((1,), (1,)), ((), ())),
             preferred_element_type=jnp.float32,
         )
         return 0
 
-    lax.fori_loop(0, width // span, correlate, 0)
-    scale = 1.0 / 262144.0
-    lane = iota((1, LANES), 1)
-    half = receivers
-    for slot in range(16):
-        base = (slot // 8) * 16 + slot % 8
-        total = jnp.zeros((receivers + 16, LANES), jnp.float32)
-        for coarse in range(COARSE):
-            top = coarse * rows
-
-            def part(out_part, in_part):
-                col = (base + in_part * 8) * FINE
-                tile = slice(col // LANES * LANES, col // LANES * LANES + LANES)
-                first = outer[top + out_part * half : top + (out_part + 1) * half, tile]
-                low = top + 2 * half
-                own = outer[low + 8 * out_part : low + 8 * out_part + 8, tile]
-                other = outer[low + 16 + 8 * out_part : low + 24 + 8 * out_part, tile]
-                return jnp.concatenate([first, own, other], axis=0)
-
-            offset = (base * FINE) % LANES
-            real = part(0, 0) + part(1, 1)
-            imag = part(1, 0) - part(0, 1)
-            real = pltpu.roll(real, (coarse * FINE - offset) % LANES, 1)
-            imag = pltpu.roll(imag, (DELAYS + coarse * FINE - offset) % LANES, 1)
-            total = jnp.where(lane >> 4 == coarse, real, total)
-            total = jnp.where(lane >> 4 == COARSE + coarse, imag, total)
-        total = total * scale
-        tidy[slot * receivers : (slot + 1) * receivers, :] = total[:receivers]
-        corr_ref[slot * 16 : (slot + 1) * 16, :] = total[receivers:]
-    for k in range(PER_RECV):
-
-        def pick(row, _):
+    lax.fori_loop(0, width // SPAN, correlate, 0)
+    flipped[...] = jnp.transpose(outer[...])
+
+    def read(coarse, out_part, tile):
+        cols = slice(tile * LANES, (tile + 1) * LANES)
+        top = coarse * rows + receivers * out_part
+        low = coarse * rows + heard_rows + 8 * out_part
+        return jnp.concatenate(
+            [
+                flipped[top : top + receivers, cols],
+                flipped[low : low + 8, cols],
+                flipped[low + 16 : low + 24, cols],
+            ],
+            axis=0,
+        )
+
+    def store(slot, lags):
+        tidy[pl.ds(pl.multiple_of(slot * receivers, receivers), receivers), :] = lags[:receivers]
+        corr_ref[pl.ds(pl.multiple_of(slot * 16, 16), 16), :] = lags[receivers:]
+
+    by_lag(read, receivers + 16, store)
+
+    def pick(row, _):
+        for k in range(PER_RECV):
             chosen = slot_ref[row, k] * receivers + row
-            picked[pl.ds(row, 1), :] = tidy[pl.ds(chosen, 1), :]
-            return 0
-
-        lax.fori_loop(0, receivers, pick, 0, unroll=8)
-        cross_ref[:, k * LANES : (k + 1) * LANES] = picked[...]
+            picked[pl.ds(k * receivers + row, 1), :] = tidy[pl.ds(chosen, 1), :]
+        return 0
+
+    lax.fori_loop(0, receivers, pick, 0, unroll=4)
+    low = iota((1, LANES), 1) < DELAYS
+    for pair in range(PER_RECV // 2):
+        even = picked[2 * pair * receivers : (2 * pair + 1) * receivers, :]
+        odd = picked[(2 * pair + 1) * receivers : (2 * pair + 2) * receivers, :]
+        cross_ref[:, pair * LANES : (pair + 1) * LANES] = jnp.where(
+            low, even, pltpu.roll(odd, DELAYS, 1)
+        )
+        pair += PER_RECV // 2
+        cross_ref[:, pair * LANES : (pair + 1) * LANES] = jnp.where(
+            low, pltpu.roll(even, DELAYS, 1), odd
+        )
+
+    def sent(step, _):
+        copy_of(shifted, kept_ref, sems, step, step * SPAN, SPAN).wait()
+        return 0
+
+    lax.fori_loop(0, width // SPAN, sent, 0)
 
 
 def receive(slot, tap_high, tap_low, slot_rows, refs, echoes):
@@ -246,39 +303,45 @@
     width = length + LANES
     smem = pl.BlockSpec(memory_space=pltpu.SMEM)
     vmem = pl.BlockSpec(memory_space=pltpu.VMEM)
-    all_rows = rows + 32
+    products = COARSE * (rows + 32)
     return pl.pallas_call(
         receive_kernel,
         out_shape=(
             jax.ShapeDtypeStruct((rows, length), jnp.bfloat16),
             jax.ShapeDtypeStruct((receivers, PER_RECV * LANES), jnp.float32),
             jax.ShapeDtypeStruct((256, LANES), jnp.float32),
+            jax.ShapeDtypeStruct((32 * FINE, width), jnp.bfloat16),
         ),
         in_specs=[smem, vmem, vmem, vmem, vmem, vmem],
-        out_specs=(vmem, vmem, vmem),
+        out_specs=(vmem, vmem, vmem, pl.BlockSpec(memory_space=pl.ANY)),
         scratch_shapes=[
             pltpu.VMEM((32 * FINE, width), jnp.bfloat16),
             pltpu.VMEM((COARSE * rows, 32 * FINE), jnp.bfloat16),
             pltpu.VMEM((COARSE * rows, 32 * FINE), jnp.bfloat16),
-            pltpu.VMEM((all_rows, width + LANES), jnp.bfloat16),
-            pltpu.VMEM((COARSE * all_rows, 32 * FINE), jnp.float32),
+            pltpu.VMEM((rows + 32, width + LANES), jnp.bfloat16),
+            pltpu.VMEM((32 * FINE, products), jnp.float32),
+            pltpu.VMEM((products, 32 * FINE), jnp.float32),
             pltpu.VMEM((16 * receivers, LANES), jnp.float32),
-            pltpu.VMEM((receivers, LANES), jnp.float32),
+            pltpu.VMEM((PER_RECV * receivers, LANES), jnp.float32),
+            pltpu.SemaphoreType.DMA((width // SPAN,)),
         ],
-        compiler_params=pltpu.CompilerParams(vmem_limit_bytes=48 * 2**20),
+        compiler_params=pltpu.CompilerParams(vmem_limit_bytes=RECEIVE_VMEM),
         name="receive",
     )(slot, tap_high, tap_low, slot_rows, refs, echoes)
 
 
-def cancel_kernel(tap_ref, slot_rows_ref, refs_ref, received_ref, out_ref, shifted, taps):
+def cancel_kernel(
+    tap_ref, slot_rows_ref, kept_ref, received_ref, out_ref, taps, shifted, sems
+):
     receivers = received_ref.shape[0] // 2
     length = received_ref.shape[1]
-    build_shifted(refs_ref, shifted)
+    arrive = fetch_all(kept_ref, shifted, sems, PIECE)
     taps[...] = lay_taps(tap_ref[...], slot_rows_ref[...], receivers)
-    piece = 512
+    piece = PIECE
 
     def project(step, _):
         start = pl.multiple_of(step * piece, LANES)
+        arrive(step)
         spread = jnp.dot(
             taps[...], shifted[:, pl.ds(start, LANES + piece)], preferred_element_type=jnp.float32
         )
@@ -289,21 +352,22 @@
     lax.fori_loop(0, length // piece, project, 0)
 
 
-def cancel(taps, slot_rows, refs, received):
+def cancel(taps, slot_rows, shifted, received):
     rows, length = received.shape
     vmem = pl.BlockSpec(memory_space=pltpu.VMEM)
     return pl.pallas_call(
         cancel_kernel,
         out_shape=jax.ShapeDtypeStruct((rows, length), jnp.bfloat16),
-        in_specs=[vmem] * 4,
+        in_specs=[vmem, vmem, pl.BlockSpec(memory_space=pl.ANY), vmem],
         out_specs=vmem,
         scratch_shapes=[
+            pltpu.VMEM((COARSE * rows, 32 * FINE), jnp.bfloat16),
             pltpu.VMEM((32 * FINE, length + LANES), jnp.bfloat16),
-            pltpu.VMEM((COARSE * rows, 32 * FINE), jnp.bfloat16),
+            pltpu.SemaphoreType.DMA((length // PIECE + 1,)),
         ],
-        compiler_params=pltpu.CompilerParams(vmem_limit_bytes=40 * 2**20),
+        compiler_params=pltpu.CompilerParams(vmem_limit_bytes=RECEIVE_VMEM),
         name="cancel",
-    )(taps, slot_rows, refs, received)
+    )(taps, slot_rows, shifted, received)
 
 
 def times_i(packed):
@@ -318,37 +382,45 @@
 def inverse(block):
     size = block.shape[0]
     lane = iota((1, LANES), 1)
+    low = lane & (DELAYS - 1)
     sub = iota((size, 1), 0)
     sign = jnp.where(lane < DELAYS, -1.0, 1.0)
 
     def spread(column):
-        return jnp.broadcast_to(column, (size, LANES))
-
-    col_re = spread(block[:, 0:1])
-    col_im = spread(block[:, DELAYS : DELAYS + 1])
-    for p in range(size):
-        last = p + 1 == size
-        if not last:
-            next_re = spread(block[:, p + 1 : p + 2])
-            next_im = spread(block[:, DELAYS + p + 1 : DELAYS + p + 2])
-        row = block[p : p + 1, :]
-        over = 1.0 / col_re[p : p + 1, :]
-        row = jnp.where(lane == p, 1.0, jnp.where(lane == DELAYS + p, 0.0, row))
-        turned = pltpu.roll(row, DELAYS, 1) * sign
-        row = row * over
-        turned = turned * over
-        if not last:
-            fac_re = col_re[p + 1 : p + 2, :] * over
-            fac_im = -col_im[p + 1 : p + 2, :] * over
-            next_re = next_re - col_re * fac_re + col_im * fac_im
-            next_im = next_im - col_re * fac_im - col_im * fac_re
-            next_re = jnp.where(sub == p, fac_re, next_re)
-            next_im = jnp.where(sub == p, fac_im, next_im)
-        block = jnp.where((lane & (DELAYS - 1)) == p, 0.0, block)
-        block = block - col_re * row - col_im * turned
-        block = jnp.where(sub == p, row, block)
-        if not last:
-            col_re, col_im = next_re, next_im
+        return jnp.broadcast_to(block[:, column : column + 1], (size, LANES))
+
+    for first in range(0, size, PANEL):
+        col_re = [spread(first + t) for t in range(PANEL)]
+        col_im = [spread(DELAYS + first + t) for t in range(PANEL)]
+        rows = [block[first + t : first + t + 1, :] for t in range(PANEL)]
+        turned_rows = [pltpu.roll(row, DELAYS, 1) * sign for row in rows]
+        block = jnp.where((low >= first) & (low < first + PANEL), 0.0, block)
+        for t in range(PANEL):
+            p = first + t
+            over = 1.0 / col_re[t][p : p + 1, :]
+            row = jnp.where(lane == p, 1.0, jnp.where(lane == DELAYS + p, 0.0, rows[t])) * over
+            turned = (
+                jnp.where(lane == DELAYS + p, 1.0, jnp.where(lane == p, 0.0, turned_rows[t])) * over
+            )
+            for u in range(t + 1, PANEL):
+                q = first + u
+                below_re = col_re[t][q : q + 1, :]
+                below_im = col_im[t][q : q + 1, :]
+                fac_re = below_re * over
+                fac_im = -below_im * over
+                next_re = col_re[u] - col_re[t] * fac_re + col_im[t] * fac_im
+                next_im = col_im[u] - col_re[t] * fac_im - col_im[t] * fac_re
+                col_re[u] = jnp.where(sub == p, fac_re, next_re)
+                col_im[u] = jnp.where(sub == p, fac_im, next_im)
+                rows[u] = jnp.where(low == p, 0.0, rows[u]) - below_re * row - below_im * turned
+                turned_rows[u] = (
+                    jnp.where(low == p, 0.0, turned_rows[u]) - below_re * turned + below_im * row
+                )
+            later = (low > p) & (low < first + PANEL)
+            row = jnp.where(later, 0.0, row)
+            turned = jnp.where(later, 0.0, turned)
+            block = block - col_re[t] * row - col_im[t] * turned
+            block = jnp.where(sub == p, row, block)
     return block
 
 
@@ -390,29 +462,34 @@
             if k == l:
                 block = block + jnp.where(lane == sub, loading, 0.0)
             system[k * size : (k + 1) * size, l * LANES : (l + 1) * LANES] = block
-    lane_sq = iota((LANES, LANES), 1)
-    sub_sq = iota((LANES, LANES), 0)
-    gather = jnp.where(lane_sq == (sub_sq >> 6) * size, 1.0, 0.0)
-    on_diag = (lane & (size - 1)) == sub
+    unit = jnp.where(lane == sub, 1.0, 0.0)
+
+    def eliminate(i, _):
+        mine = pl.ds(pl.multiple_of(i * size, size), size)
+        col = pl.ds(pl.multiple_of(i * LANES, LANES), LANES)
+        over = inverse(system[mine, col])
+        system[mine, col] = unit
+        right = system[mine, :]
+        scaled = exact_dot(over, jnp.concatenate([right, times_i(right)], axis=0))
+        factors = system[:, col]
+        system[:, col] = jnp.zeros((count * size, LANES), jnp.float32)
+        both = jnp.concatenate([scaled, times_i(scaled)], axis=0)
+        system[...] = system[...] - exact_dot(factors, both)
+        system[mine, :] = scaled
+        return 0
+
+    lax.fori_loop(0, count, eliminate, 0)
+    whole = count * size
+    total = cross_ref[...]
+    sides = jnp.concatenate(
+        [total[:, :whole], total[:, whole:], jnp.zeros((6, whole), jnp.float32)], axis=0
+    )
+    found = exact_dot(sides, system[...])
     for k in range(count):
-        spread = jnp.where(on_diag, cross_ref[:, k * LANES : (k + 1) * LANES], 0.0)
-        system[k * size : (k + 1) * size, count * LANES :] = exact_dot(spread, gather)
-    for i in range(count):
-        mine = slice(i * size, (i + 1) * size)
-        col = slice(i * LANES, (i + 1) * LANES)
-        rest = slice((i + 1) * LANES, (count + 1) * LANES)
-        over = inverse(system[mine, col])
-        right = system[mine, rest]
-        scaled = exact_dot(over, jnp.concatenate([right, times_i(right)], axis=0))
-        both = jnp.concatenate([scaled, times_i(scaled)], axis=0)
-        system[:, rest] = system[:, rest] - exact_dot(system[:, col], both)
-        system[mine, rest] = scaled
-    scatter = jnp.where(sub_sq == (lane_sq >> 6) * size, 1.0, 0.0)
-    ones = jnp.ones((8, size), jnp.float32)
-    for k in range(count):
-        found = exact_dot(system[k * size : (k + 1) * size, count * LANES :], scatter)
-        row = exact_dot(ones, jnp.where(on_diag, found, 0.0))
-        out_ref[:, k * LANES : (k + 1) * LANES] = row[0:1]
+        by_real = found[0:1, k * LANES : (k + 1) * LANES]
+        by_imag = found[1:2, k * LANES : (k + 1) * LANES]
+        row = jnp.where(lane < size, by_real, -by_real) + pltpu.roll(by_imag, size, 1)
+        out_ref[:, k * LANES : (k + 1) * LANES] = row
 
 
 def solve(slot, corr, cross):
@@ -425,9 +502,10 @@
         in_specs=[smem, vmem, vmem],
         out_specs=vmem,
         scratch_shapes=[
-            pltpu.VMEM((size, (PER_RECV + 1) * LANES), jnp.float32),
+            pltpu.VMEM((size, PER_RECV * LANES), jnp.float32),
             pltpu.VMEM((40, 2 * LANES), jnp.float32),
         ],
+        compiler_params=pltpu.CompilerParams(vmem_limit_bytes=RECEIVE_VMEM),
         name="solve",
     )(slot, corr, cross)
 
@@ -460,8 +538,13 @@
     )
     tap_high = lax.reduce_precision(gain_taps, 8, 7)
     tap_low = (gain_taps - tap_high).astype(jnp.bfloat16)
-    received, cross, corr = receive(
-        slot, tap_high.astype(jnp.bfloat16), tap_low, slot_rows, refs, echoes.reshape(2 * recv_count, length)
+    received, cross, corr, shifted = receive(
+        slot,
+        tap_high.astype(jnp.bfloat16),
+        tap_low,
+        slot_rows,
+        refs,
+        echoes.reshape(2 * recv_count, length),
     )
     share = recv_count // tm_count
     corr_share = corr.size // tm_count
@@ -471,15 +554,15 @@
     my_corr = jnp.broadcast_to(parts[:, PER_RECV * LANES :], (tm_count, corr_share))
     corr = lax.all_to_all(my_corr, "tm", 0, 0, tiled=True).reshape(256, LANES)
     my_slot = lax.dynamic_slice_in_dim(slot, tm_index * share, share, 0).reshape(PER_RECV)
-    mine = solve(my_slot, corr, my_cross)
-    solved = lax.all_to_all(
-        jnp.broadcast_to(mine, (tm_count, PER_RECV * LANES)), "tm", 0, 0, tiled=True
-    ).reshape(recv_count, PER_RECV, 2, DELAYS)
+    mine = jnp.broadcast_to(solve(my_slot, corr, my_cross), (tm_count, PER_RECV * LANES))
+    solved = lax.all_to_all(mine, "tm", 0, 0, tiled=True).reshape(
+        recv_count, PER_RECV, 2, DELAYS
+    )
     weights = jnp.transpose(solved, (2, 0, 1, 3)).reshape(2, recv_count, PER_RECV * DELAYS)
     taps = jnp.transpose(solved.astype(jnp.bfloat16), (1, 0, 2, 3)).reshape(
         PER_RECV * recv_count, LANES
     )
-    cancelled = cancel(taps, slot_rows, refs, received).reshape(2, recv_count, length)
+    cancelled = cancel(taps, slot_rows, shifted, received).reshape(2, recv_count, length)
     return (cancelled, weights)
 
 

time: 146 us -> 140 us (0.959)
  Pallas kernels: 77.8 us -> 67.7 us
  other arithmetic: 2.9 us -> 5.81 us
  local copies, waits for them, and re-layouts: 5.27 us -> 8.12 us
  waiting for transfers between devices: 11.3 us -> 9.5 us
    pallas_call x1, Pallas kernels: 41.2 us -> 33.2 us  [solve(): pl.pallas_call(solve_kernel, out_shape=jax.ShapeDtypeStruct((1, PER_RECV...]
    pallas_call x1, Pallas kernels: 12.5 us -> 8.69 us  [cancel(): pl.pallas_call(cancel_kernel, out_shape=jax.ShapeDtypeStruct((rows, lengt...]
    pallas_call x1, Pallas kernels: 24.1 us -> 25.8 us  [receive(): pl.pallas_call(receive_kernel, out_shape=(jax.ShapeDtypeStruct((rows, len...]
  transfers between devices with their start and end apart: 3 -> 3, of which waited for: 3 -> 3; matrix products, arithmetic and copies ran while one was open for 1% -> 3% of each run, Pallas kernels for 0% -> 0%
where the time goes in v2:
time: 140 us; the launch traced here: 139 us
  Pallas kernels  67.7 us (48%)
  blocking collectives  27.7 us (20%)
  starting transfers between devices  14.8 us (11%)
  waiting for transfers between devices  9.5 us (7%)
  local copies, waits for them, and re-layouts  8.12 us (6%)
  other arithmetic  5.81 us (4%)
  matrix products  4.62 us (3%)
    pallas_call x1, Pallas kernels, solve(): pl.pallas_call(solve_kernel, out_shape=jax.ShapeDtypeStruct((1, PER_RECV...  33.2 us
    pallas_call x1, Pallas kernels, receive(): pl.pallas_call(receive_kernel, out_shape=(jax.ShapeDtypeStruct((rows, len...  25.8 us
    all_to_all x1, blocking collectives, local(): lax.all_to_all(parts, 'tm', 0, 0, tiled=True)  16.6 us
    all_to_all x1, blocking collectives, local(): lax.all_to_all(mine, 'tm', 0, 0, tiled=True)  11 us
    pallas_call x1, Pallas kernels, cancel(): pl.pallas_call(cancel_kernel, out_shape=jax.ShapeDtypeStruct((rows, lengt...  8.69 us
    ppermute x1, starting transfers between devices, passed_along(): lax.ppermute(array, axis, [(i, (i + by) % peers) for i in range(peers)])  6.46 us
    all_to_all x1, waiting for transfers between devices, local(): corr = lax.all_to_all(my_corr, 'tm', 0, 0, tiled=True).reshape(256, LANES)  5.7 us
    ppermute x1, starting transfers between devices, from_behind(): return lax.ppermute(block, axis, route)  4.51 us
  transfers between devices with their start and end apart: 3, of which 3 were waited for; matrix products, arithmetic and copies ran while one was open for 3% of the time, Pallas kernels for 0%

profile of v2, /device:TPU:1, one launch (start us, length us, event | category | flops | bytes accessed | tf_op | source)
XLA Modules:
  0.0 139.3 jit_solution(6767487069634974968)
XLA Ops:
  0.8 1.2 fusion.8
  6.5 0.6 fusion.1
  7.6 6.5 %collective-permute-start = (bf16[16,8192]{1,0:T(8,128)(2,1)S(1)}, bf16[16,8192]{1,0:T(8,128)(2,1)S(1)}, u32[]{:S(2)}, u32[]{:S(2)}) collective-permute-start(bf16[16,8192]{1,0:T(8,128)(2,1)S(1)} %maximum_bitcast_fusion), channel_id=1, source_target_pairs={{0,224},{32,0},{64,32},{96,64},{128,96},{160,128},{192,160},{224,1... | collective-permute-start | bytes 786440 | tf_op jit(solution)/shard_map/ppermute | solution.py:28
  14.2 0.6 fusion.68.slot_ref
  15.1 0.8 fusion.22
  15.9 3.2 %collective-permute-done = bf16[16,8192]{1,0:T(8,128)(2,1)S(1)} collective-permute-done((bf16[16,8192]{1,0:T(8,128)(2,1)S(1)}, bf16[16,8192]{1,0:T(8,128)(2,1)S(1)}, u32[]{:S(2)}, u32[]{:S(2)}) %collective-permute-start) | collective-permute-done | bytes 262176 | tf_op jit(solution)/shard_map/ppermute | solution.py:28
  19.1 4.5 %collective-permute-start.1 = (bf16[32,128]{1,0:T(8,128)(2,1)S(1)}, bf16[32,128]{1,0:T(8,128)(2,1)S(1)}, u32[]{:S(2)}, u32[]{:S(2)}) collective-permute-start(bf16[32,128]{1,0:T(8,128)(2,1)S(1)} %pad_maximum_fusion.1), channel_id=1, source_target_pairs={{0,1},{1,2},{2,3},{3,4},{4,5},{5,6},{6,7},{7,8},{8,9},{9,10},{10,1... | collective-permute-start | bytes 24584 | tf_op jit(solution)/shard_map/ppermute | solution.py:34
  24.4 0.8 maximum_maximum_fusion.refs_ref
  25.2 0.7 broadcast_in_dim.70.slot_rows_ref
  26.0 25.8 %receive.1 = (bf16[64,8192]{1,0:T(8,128)(2,1)}, f32[32,768]{1,0:T(8,128)}, f32[256,128]{1,0:T(8,128)}, bf16[512,8320]{1,0:T(8,128)(2,1)}) custom-call(s32[32,6]{1,0:T(8,128)} %fusion.68.slot_ref, bf16[192,128]{1,0:T(8,128)(2,1)} %get-tuple-element.17.tap_high_ref, bf16[192,128]{1,0:T(8,128)(2,1)} %get-tuple-element.16.tap_low_ref, ...), custom_call_target="tpu_custom_call" | custom-call | tf_op jit(solution)/shard_map/receive/pallas_call | solution.py:307
  51.8 0.9 reshape.195
  52.7 0.9 pad_maximum_fusion
  53.8 16.6 %all_to_all.21 = f32[32,1,1792]{2,1,0:T(1,128)S(1)} all-to-all(f32[32,1,1792]{2,1,0:T(1,128)S(1)} %all_to_all.14), channel_id=1, replica_groups=mesh['chan'=8,'tm'=32] {'tm'}, dimensions={0} | all-to-all | bytes 458752 | tf_op jit(solution)/shard_map/all_to_all | solution.py:552
  70.6 0.7 broadcast_in_dim.72
  71.3 3.8 %all-to-all-start.1 = ((f32[32,1,1024]{2,1,0:T(1,128)}), f32[32,1,1024]{2,1,0:T(1,128)S(1)}, u32[]{:S(2)}, u32[]{:S(2)}) async-start(f32[32,1,1024]{2,1,0:T(1,128)} %broadcast_in_dim.72), calls=%async_computation.1 | async-start | bytes 262144 | tf_op jit(solution)/shard_map/all_to_all | solution.py:555
  75.2 1.3 dynamic-slice_bitcast_fusion.slot_ref
  77.0 5.7 %all-to-all-done.1 = f32[32,1,1024]{2,1,0:T(1,128)S(1)} async-done(((f32[32,1,1024]{2,1,0:T(1,128)}), f32[32,1,1024]{2,1,0:T(1,128)S(1)}, u32[]{:S(2)}, u32[]{:S(2)}) %all-to-all-start.1) | async-done | bytes 131104 | tf_op jit(solution)/shard_map/all_to_all | solution.py:555
  82.7 0.7 copy-done
  83.4 33.2 %solve.1 = f32[1,768]{1,0:T(1,128)} custom-call(s32[6]{0:T(128)} %dynamic-slice_bitcast_fusion.slot_ref, f32[256,128]{1,0:T(8,128)} %bitcast.57, f32[1,768]{1,0:T(1,128)} %slice.24.cross_ref), custom_call_target="tpu_custom_call" | custom-call | tf_op jit(solution)/shard_map/solve/pallas_call | solution.py:499
  116.6 0.7 reduce.1
  117.3 11.0 %all_to_all.22 = f32[32,1,768]{2,1,0:T(1,128)S(1)} all-to-all(f32[32,1,768]{2,1,0:T(1,128)S(1)} %broadcast_in_dim.73), channel_id=1, replica_groups=mesh['chan'=8,'tm'=32] {'tm'}, dimensions={0} | all-to-all | bytes 196608 | tf_op jit(solution)/shard_map/all_to_all | solution.py:558
  128.9 0.7 reshape.198.tap_ref
  129.7 0.7 reshape.200
  130.4 8.7 %cancel.1 = bf16[64,8192]{1,0:T(8,128)(2,1)} custom-call(bf16[192,128]{1,0:T(8,128)(2,1)} %reshape.198.tap_ref, s32[192,128]{1,0:T(8,128)} %broadcast_in_dim.70.slot_rows_ref, bf16[512,8320]{1,0:T(8,128)(2,1)} %get-tuple-element.8.kept_ref, bf16[64,8192]{1,0:T(8,128)(2,1)} %get-tuple-element.9.received_ref), custom_call_target="tpu_custom_call" | custom-call | tf_op jit(solution)/shard_map/cancel/pallas_call | solution.py:358
  (47 shorter events, 7.6 us)
Async XLA Ops:
  7.3 6.8 %copy-start.1 = (f32[2,32,6]{1,0,2:T(2,128)S(1)}, f32[2,32,6]{1,0,2:T(2,128)}, u32[]{:S(2)}) copy-start(f32[2,32,6]{1,0,2:T(2,128)} %param.8) | copy-start | bytes 4612
  7.4 6.8 %copy-start.2 = (s32[32,6]{0,1:T(8,128)S(1)}, s32[32,6]{0,1:T(8,128)}, u32[]{:S(2)}) copy-start(s32[32,6]{0,1:T(8,128)} %param.6) | copy-start | bytes 2308
  7.4 7.5 %copy-start.3 = (s32[32,6]{0,1:T(8,128)S(1)}, s32[32,6]{0,1:T(8,128)}, u32[]{:S(2)}) copy-start(s32[32,6]{0,1:T(8,128)} %param.7) | copy-start | bytes 2308
  7.6 11.5 %collective-permute-start = (bf16[16,8192]{1,0:T(8,128)(2,1)S(1)}, bf16[16,8192]{1,0:T(8,128)(2,1)S(1)}, u32[]{:S(2)}, u32[]{:S(2)}) collective-permute-start(bf16[16,8192]{1,0:T(8,128)(2,1)S(1)} %maximum_bitcast_fusion), channel_id=1, source_target_pairs={{0,224},{32,0},{64,32},{96,64},{128,96},{160,128},{192,160},{224,1... | collective-permute-start | bytes 786440 | tf_op jit(solution)/shard_map/ppermute | solution.py:28
  19.1 5.3 %collective-permute-start.1 = (bf16[32,128]{1,0:T(8,128)(2,1)S(1)}, bf16[32,128]{1,0:T(8,128)(2,1)S(1)}, u32[]{:S(2)}, u32[]{:S(2)}) collective-permute-start(bf16[32,128]{1,0:T(8,128)(2,1)S(1)} %pad_maximum_fusion.1), channel_id=1, source_target_pairs={{0,1},{1,2},{2,3},{3,4},{4,5},{5,6},{6,7},{7,8},{8,9},{9,10},{10,1... | collective-permute-start | bytes 24584 | tf_op jit(solution)/shard_map/ppermute | solution.py:34
  71.3 11.4 %all-to-all-start.1 = ((f32[32,1,1024]{2,1,0:T(1,128)}), f32[32,1,1024]{2,1,0:T(1,128)S(1)}, u32[]{:S(2)}, u32[]{:S(2)}) async-start(f32[32,1,1024]{2,1,0:T(1,128)} %broadcast_in_dim.72), calls=%async_computation.1 | async-start | bytes 262144 | tf_op jit(solution)/shard_map/all_to_all | solution.py:555
  82.7 0.7 copy-start

commit v3 on v2

--- a/solution.py
+++ b/solution.py
@@ -13,9 +13,10 @@
 LANES = 128
 FINE = 16
 COARSE = DELAYS // FINE
+PARTS = PER_RECV * LANES + 1024
 PANEL = 4
-SPAN = 640
-PIECE = 1024
+SPAN = 1664
+PIECE = 2048
 RECEIVE_VMEM = 56 * 2**20
 
 
@@ -127,30 +128,67 @@
     lax.fori_loop(0, width // piece, one_piece, 0)
 
 
-def lay_taps(tap_rows, slot_rows, receivers):
-    cols = 32 * FINE
-    lane = iota((LANES, cols), 1)
-    source = iota((LANES, cols), 0)
-    fine = lane & (FINE - 1)
-    in_part = (lane >> 7) & 1
-    col_slot = ((iota((1, cols), 1) >> 8) << 3) + ((iota((1, cols), 1) >> 4) & 7)
-    blocks = []
-    for coarse in range(COARSE):
-        for out_part in range(2):
-            part = in_part ^ out_part
-            sign = jnp.where((in_part == 1) & (out_part == 0), -1.0, 1.0)
-            spread = jnp.where(source == part * DELAYS + coarse * FINE + fine, sign, 0.0)
-            wide = jnp.dot(
-                tap_rows, spread.astype(jnp.bfloat16), preferred_element_type=jnp.float32
-            )
-            total = jnp.zeros((receivers, cols), jnp.float32)
-            for k in range(PER_RECV):
-                rows = slice(k * receivers, (k + 1) * receivers)
-                total = total + jnp.where(
-                    slot_rows[rows, 0:1] == col_slot, wide[rows, :], 0.0
-                )
-            blocks.append(total)
-    return jnp.concatenate(blocks, axis=0).astype(jnp.bfloat16)
+def lay_taps(tap_rows, slot_rows, receivers, sets):
+    lane = iota((LANES, LANES), 1)
+    source = iota((LANES, LANES), 0)
+    spread = jnp.concatenate(
+        [
+            jnp.where(source == part * DELAYS + coarse * FINE + (lane & (FINE - 1)), 1.0, 0.0)
+            for coarse in range(COARSE)
+            for part in range(2)
+        ],
+        axis=1,
+    )
+    wide = jnp.dot(tap_rows, spread.astype(jnp.bfloat16), preferred_element_type=jnp.float32)
+    here = iota((1, LANES), 1) >> 4
+    count = PER_RECV * receivers
+    seen = [
+        [slot_rows[k * receivers : (k + 1) * receivers, :] == half * 8 + here for half in range(2)]
+        for k in range(PER_RECV)
+    ]
+    laid = []
+    for which in range(sets):
+        blocks = []
+        for coarse in range(COARSE):
+            for out_part in range(2):
+                tiles = []
+                for half in range(2):
+                    for in_part in range(2):
+                        tile = (coarse * 2 + (in_part ^ out_part)) * LANES
+                        total = jnp.zeros((receivers, LANES), jnp.float32)
+                        for k in range(PER_RECV):
+                            top = which * count + k * receivers
+                            total = jnp.where(
+                                seen[k][half],
+                                total + wide[top : top + receivers, tile : tile + LANES],
+                                total,
+                            )
+                        tiles.append(-total if in_part == 1 and out_part == 0 else total)
+                blocks.append(jnp.concatenate(tiles, axis=1))
+        laid.append(jnp.concatenate(blocks, axis=0).astype(jnp.bfloat16))
+    return laid
+
+
+def lay_gains_kernel(tap_ref, slot_rows_ref, out_ref):
+    receivers = slot_rows_ref.shape[0] // PER_RECV
+    high, low = lay_taps(tap_ref[...], slot_rows_ref[...], receivers, 2)
+    rows = high.shape[0]
+    out_ref[0:rows, :] = high
+    out_ref[rows:, :] = low
+
+
+def lay_gains(taps, slot_rows):
+    vmem = pl.BlockSpec(memory_space=pltpu.VMEM)
+    receivers = slot_rows.shape[0] // PER_RECV
+    return pl.pallas_call(
+        lay_gains_kernel,
+        out_shape=jax.ShapeDtypeStruct((4 * COARSE * receivers, 32 * FINE), jnp.bfloat16),
+        in_specs=[vmem, vmem],
+        out_specs=vmem,
+        compiler_params=pltpu.CompilerParams(vmem_limit_bytes=16 * 2**20),
+        cost_estimate=pl.CostEstimate(flops=10**9, bytes_accessed=10**6, transcendentals=0),
+        name="lay_gains",
+    )(taps, slot_rows)
 
 
 def coarse_sum(spread):
@@ -208,18 +246,17 @@
 
 
 def receive_kernel(
-    slot_ref, tap_high_ref, tap_low_ref, slot_rows_ref, refs_ref, echo_ref,
-    received_ref, cross_ref, corr_ref, kept_ref,
-    shifted, taps_high, taps_low, signal, outer, flipped, tidy, picked, sems,
+    slot_ref, taps_ref, refs_ref, echo_ref,
+    received_ref, parts_ref, kept_ref,
+    shifted, signal, outer, flipped, tidy, picked, corr, sems,
 ):
     receivers = echo_ref.shape[0] // 2
     length = echo_ref.shape[1]
     width = length + LANES
     heard_rows = 2 * receivers
     rows = heard_rows + 32
+    groups = COARSE * heard_rows
     build_shifted(refs_ref, shifted, kept_ref, sems)
-    taps_high[...] = lay_taps(tap_high_ref[...], slot_rows_ref[...], receivers)
-    taps_low[...] = lay_taps(tap_low_ref[...], slot_rows_ref[...], receivers)
     signal[:, 0:LANES] = jnp.zeros((rows, LANES), jnp.bfloat16)
     signal[heard_rows:rows, LANES:width] = refs_ref[:, LANES:width]
     signal[:, width : width + LANES] = jnp.zeros((rows, LANES), jnp.bfloat16)
@@ -227,9 +264,9 @@
     def direct(step, _):
         start = pl.multiple_of(step * PIECE, LANES)
         window = shifted[:, pl.ds(start, LANES + PIECE)]
-        spread = jnp.dot(taps_high[...], window, preferred_element_type=jnp.float32) + jnp.dot(
-            taps_low[...], window, preferred_element_type=jnp.float32
-        )
+        spread = jnp.dot(
+            taps_ref[0:groups, :], window, preferred_element_type=jnp.float32
+        ) + jnp.dot(taps_ref[groups:, :], window, preferred_element_type=jnp.float32)
         echo = echo_ref[:, pl.ds(start, PIECE)].astype(jnp.float32)
         heard = (echo + coarse_sum(spread)).astype(jnp.bfloat16)
         received_ref[:, pl.ds(start, PIECE)] = heard
@@ -267,7 +304,7 @@
 
     def store(slot, lags):
         tidy[pl.ds(pl.multiple_of(slot * receivers, receivers), receivers), :] = lags[:receivers]
-        corr_ref[pl.ds(pl.multiple_of(slot * 16, 16), 16), :] = lags[receivers:]
+        corr[pl.ds(pl.multiple_of(slot * 16, 16), 16), :] = lags[receivers:]
 
     by_lag(read, receivers + 16, store)
 
@@ -282,13 +319,17 @@
     for pair in range(PER_RECV // 2):
         even = picked[2 * pair * receivers : (2 * pair + 1) * receivers, :]
         odd = picked[(2 * pair + 1) * receivers : (2 * pair + 2) * receivers, :]
-        cross_ref[:, pair * LANES : (pair + 1) * LANES] = jnp.where(
+        parts_ref[:, pair * LANES : (pair + 1) * LANES] = jnp.where(
             low, even, pltpu.roll(odd, DELAYS, 1)
         )
         pair += PER_RECV // 2
-        cross_ref[:, pair * LANES : (pair + 1) * LANES] = jnp.where(
+        parts_ref[:, pair * LANES : (pair + 1) * LANES] = jnp.where(
             low, pltpu.roll(even, DELAYS, 1), odd
         )
+    each = 256 // receivers
+    for row in range(each):
+        tile = PER_RECV + row
+        parts_ref[:, tile * LANES : (tile + 1) * LANES] = corr[pl.ds(row, receivers, stride=each), :]
 
     def sent(step, _):
         copy_of(shifted, kept_ref, sems, step, step * SPAN, SPAN).wait()
@@ -297,7 +338,7 @@
     lax.fori_loop(0, width // SPAN, sent, 0)
 
 
-def receive(slot, tap_high, tap_low, slot_rows, refs, echoes):
+def receive(slot, taps, refs, echoes):
     rows, length = echoes.shape
     receivers = rows // 2
     width = length + LANES
@@ -308,35 +349,44 @@
         receive_kernel,
         out_shape=(
             jax.ShapeDtypeStruct((rows, length), jnp.bfloat16),
-            jax.ShapeDtypeStruct((receivers, PER_RECV * LANES), jnp.float32),
-            jax.ShapeDtypeStruct((256, LANES), jnp.float32),
+            jax.ShapeDtypeStruct((receivers, PARTS), jnp.float32),
             jax.ShapeDtypeStruct((32 * FINE, width), jnp.bfloat16),
         ),
-        in_specs=[smem, vmem, vmem, vmem, vmem, vmem],
-        out_specs=(vmem, vmem, vmem, pl.BlockSpec(memory_space=pl.ANY)),
+        in_specs=[smem, vmem, vmem, vmem],
+        out_specs=(vmem, vmem, pl.BlockSpec(memory_space=pl.ANY)),
         scratch_shapes=[
             pltpu.VMEM((32 * FINE, width), jnp.bfloat16),
-            pltpu.VMEM((COARSE * rows, 32 * FINE), jnp.bfloat16),
-            pltpu.VMEM((COARSE * rows, 32 * FINE), jnp.bfloat16),
             pltpu.VMEM((rows + 32, width + LANES), jnp.bfloat16),
             pltpu.VMEM((32 * FINE, products), jnp.float32),
             pltpu.VMEM((products, 32 * FINE), jnp.float32),
             pltpu.VMEM((16 * receivers, LANES), jnp.float32),
             pltpu.VMEM((PER_RECV * receivers, LANES), jnp.float32),
+            pltpu.VMEM((256, LANES), jnp.float32),
             pltpu.SemaphoreType.DMA((width // SPAN,)),
         ],
         compiler_params=pltpu.CompilerParams(vmem_limit_bytes=RECEIVE_VMEM),
         name="receive",
-    )(slot, tap_high, tap_low, slot_rows, refs, echoes)
+    )(slot, taps, refs, echoes)
 
 
 def cancel_kernel(
-    tap_ref, slot_rows_ref, kept_ref, received_ref, out_ref, taps, shifted, sems
+    solved_ref, slot_rows_ref, kept_ref, received_ref, out_ref, weights_ref, taps, shifted, sems
 ):
     receivers = received_ref.shape[0] // 2
     length = received_ref.shape[1]
     arrive = fetch_all(kept_ref, shifted, sems, PIECE)
-    taps[...] = lay_taps(tap_ref[...], slot_rows_ref[...], receivers)
+    whole = PER_RECV * DELAYS
+    weights_ref[0] = solved_ref[:, :whole]
+    weights_ref[1] = solved_ref[:, whole:]
+    low = iota((1, LANES), 1) < DELAYS
+    rows = []
+    for pair in range(PER_RECV // 2):
+        real = solved_ref[:, pair * LANES : (pair + 1) * LANES]
+        imag = solved_ref[:, whole + pair * LANES : whole + (pair + 1) * LANES]
+        rows.append(jnp.where(low, real, pltpu.roll(imag, DELAYS, 1)))
+        rows.append(jnp.where(low, pltpu.roll(real, DELAYS, 1), imag))
+    tap_rows = jnp.concatenate(rows, axis=0).astype(jnp.bfloat16)
+    taps[...] = lay_taps(tap_rows, slot_rows_ref[...], receivers, 1)[0]
     piece = PIECE
 
     def project(step, _):
@@ -352,14 +402,18 @@
     lax.fori_loop(0, length // piece, project, 0)
 
 
-def cancel(taps, slot_rows, shifted, received):
+def cancel(solved, slot_rows, shifted, received):
     rows, length = received.shape
+    whole = PER_RECV * DELAYS
     vmem = pl.BlockSpec(memory_space=pltpu.VMEM)
     return pl.pallas_call(
         cancel_kernel,
-        out_shape=jax.ShapeDtypeStruct((rows, length), jnp.bfloat16),
+        out_shape=(
+            jax.ShapeDtypeStruct((rows, length), jnp.bfloat16),
+            jax.ShapeDtypeStruct((2, rows // 2, whole), jnp.float32),
+        ),
         in_specs=[vmem, vmem, pl.BlockSpec(memory_space=pl.ANY), vmem],
-        out_specs=vmem,
+        out_specs=(vmem, vmem),
         scratch_shapes=[
             pltpu.VMEM((COARSE * rows, 32 * FINE), jnp.bfloat16),
             pltpu.VMEM((32 * FINE, length + LANES), jnp.bfloat16),
@@ -367,7 +421,7 @@
         ],
         compiler_params=pltpu.CompilerParams(vmem_limit_bytes=RECEIVE_VMEM),
         name="cancel",
-    )(taps, slot_rows, shifted, received)
+    )(solved, slot_rows, shifted, received)
 
 
 def times_i(packed):
@@ -485,27 +539,35 @@
         [total[:, :whole], total[:, whole:], jnp.zeros((6, whole), jnp.float32)], axis=0
     )
     found = exact_dot(sides, system[...])
+    rows = []
     for k in range(count):
         by_real = found[0:1, k * LANES : (k + 1) * LANES]
         by_imag = found[1:2, k * LANES : (k + 1) * LANES]
-        row = jnp.where(lane < size, by_real, -by_real) + pltpu.roll(by_imag, size, 1)
-        out_ref[:, k * LANES : (k + 1) * LANES] = row
-
-
-def solve(slot, corr, cross):
+        rows.append(jnp.where(lane < size, by_real, -by_real) + pltpu.roll(by_imag, size, 1))
+    for pair in range(count // 2):
+        even, odd = rows[2 * pair], rows[2 * pair + 1]
+        real = jnp.where(lane < size, even, pltpu.roll(odd, size, 1))
+        imag = jnp.where(lane < size, pltpu.roll(even, size, 1), odd)
+        low, high = pair * LANES, whole + pair * LANES
+        shape = (out_ref.shape[0], LANES)
+        out_ref[:, low : low + LANES] = jnp.broadcast_to(real, shape)
+        out_ref[:, high : high + LANES] = jnp.broadcast_to(imag, shape)
+
+
+def solve(slot, corr, cross, peers):
     smem = pl.BlockSpec(memory_space=pltpu.SMEM)
     vmem = pl.BlockSpec(memory_space=pltpu.VMEM)
     size = PER_RECV * DELAYS
     return pl.pallas_call(
         solve_kernel,
-        out_shape=jax.ShapeDtypeStruct((1, PER_RECV * LANES), jnp.float32),
+        out_shape=jax.ShapeDtypeStruct((peers, PER_RECV * LANES), jnp.float32),
         in_specs=[smem, vmem, vmem],
         out_specs=vmem,
         scratch_shapes=[
             pltpu.VMEM((size, PER_RECV * LANES), jnp.float32),
             pltpu.VMEM((40, 2 * LANES), jnp.float32),
         ],
-        compiler_params=pltpu.CompilerParams(vmem_limit_bytes=RECEIVE_VMEM),
+        compiler_params=pltpu.CompilerParams(vmem_limit_bytes=16 * 2**20),
         name="solve",
     )(slot, corr, cross)
 
@@ -519,9 +581,15 @@
     recv_count = echoes.shape[1]
     own = remodulate(symbols).reshape(2 * owned, length)
     following = passed_along(own, "chan", -1)
-    window = jnp.concatenate([own, following], axis=0)
-    previous = from_behind(window[:, length - LANES :], "tm", 1)
-    refs = jnp.concatenate([previous, window], axis=1)
+    own_halo = from_behind(own[:, length - LANES :], "tm", 1)
+    next_halo = passed_along(own_halo, "chan", -1)
+    refs = jnp.concatenate(
+        [
+            jnp.concatenate([own_halo, own], axis=1),
+            jnp.concatenate([next_halo, following], axis=1),
+        ],
+        axis=0,
+    )
     owner_chan = incidence // owned
     slot = (owner_chan - chan_index) % chan_count * owned + incidence % owned
     slot_rows = jnp.broadcast_to(
@@ -538,32 +606,20 @@
     )
     tap_high = lax.reduce_precision(gain_taps, 8, 7)
     tap_low = (gain_taps - tap_high).astype(jnp.bfloat16)
-    received, cross, corr, shifted = receive(
-        slot,
-        tap_high.astype(jnp.bfloat16),
-        tap_low,
-        slot_rows,
-        refs,
-        echoes.reshape(2 * recv_count, length),
-    )
+    gain_rows = jnp.concatenate([tap_high.astype(jnp.bfloat16), tap_low], axis=0)
+    laid = lay_gains(gain_rows, slot_rows)
+    received, parts, shifted = receive(slot, laid, refs, echoes.reshape(2 * recv_count, length))
     share = recv_count // tm_count
-    corr_share = corr.size // tm_count
-    parts = jnp.concatenate([cross, corr.reshape(tm_count, corr_share)], axis=1)
+    corr_share = 256 * LANES // tm_count
     parts = jnp.sum(lax.all_to_all(parts, "tm", 0, 0, tiled=True), axis=0, keepdims=True)
     my_cross = parts[:, : PER_RECV * LANES]
     my_corr = jnp.broadcast_to(parts[:, PER_RECV * LANES :], (tm_count, corr_share))
     corr = lax.all_to_all(my_corr, "tm", 0, 0, tiled=True).reshape(256, LANES)
     my_slot = lax.dynamic_slice_in_dim(slot, tm_index * share, share, 0).reshape(PER_RECV)
-    mine = jnp.broadcast_to(solve(my_slot, corr, my_cross), (tm_count, PER_RECV * LANES))
-    solved = lax.all_to_all(mine, "tm", 0, 0, tiled=True).reshape(
-        recv_count, PER_RECV, 2, DELAYS
-    )
-    weights = jnp.transpose(solved, (2, 0, 1, 3)).reshape(2, recv_count, PER_RECV * DELAYS)
-    taps = jnp.transpose(solved.astype(jnp.bfloat16), (1, 0, 2, 3)).reshape(
-        PER_RECV * recv_count, LANES
-    )
-    cancelled = cancel(taps, slot_rows, shifted, received).reshape(2, recv_count, length)
-    return (cancelled, weights)
+    mine = solve(my_slot, corr, my_cross, tm_count)
+    solved = lax.all_to_all(mine, "tm", 0, 0, tiled=True)
+    cancelled, weights = cancel(solved, slot_rows, shifted, received)
+    return (cancelled.reshape(2, recv_count, length), weights)
 
 
 def solution(mesh):

time: 140 us -> 126 us (0.900)
  Pallas kernels: 67.7 us -> 60.2 us
  other arithmetic: 5.81 us -> 3.29 us
  waiting for transfers between devices: 9.5 us -> 7.08 us
  local copies, waits for them, and re-layouts: 8.12 us -> 5.72 us
    pallas_call x1, Pallas kernels: 25.8 us -> 19.9 us  [receive(): pl.pallas_call(receive_kernel, out_shape=(jax.ShapeDtypeStruct((rows, len...]
    ppermute x1 -> x2, waiting for transfers between devices: 3.22 us -> 0.18 us  [passed_along(): lax.ppermute(array, axis, [(i, (i + by) % peers) for i in range(peers)])]
    reshape x4 -> x0, local copies, waits for them, and re-layouts: 2.56 us -> none  [the longest x1 0.93 us: local(): parts = jnp.concatenate([cross, corr.reshape(tm_count, corr_share)], axis=1)]
    pallas_call x2 -> x3, Pallas kernels: 41.9 us -> 40.2 us  [the longest x1 32.3 us: solve(): pl.pallas_call(solve_kernel, out_shape=jax.ShapeDtypeStruct((peers, PER_R...]
    ppermute x1 -> x2, starting transfers between devices: 6.46 us -> 7.22 us  [passed_along(): lax.ppermute(array, axis, [(i, (i + by) % peers) for i in range(peers)])]
  transfers between devices with their start and end apart: 3 -> 4, of which waited for: 3 -> 2; matrix products, arithmetic and copies ran while one was open for 3% -> 2% of each run, Pallas kernels for 0% -> 0%
where the time goes in v3:
time: 126 us; the launch traced here: 125 us
  Pallas kernels  60.2 us (48%)
  blocking collectives  28.1 us (22%)
  starting transfers between devices  15.1 us (12%)
  waiting for transfers between devices  7.08 us (6%)
  local copies, waits for them, and re-layouts  5.72 us (5%)
  matrix products  4.62 us (4%)
  other arithmetic  3.29 us (3%)
    pallas_call x1, Pallas kernels, solve(): pl.pallas_call(solve_kernel, out_shape=jax.ShapeDtypeStruct((peers, PER_R...  32.3 us
    pallas_call x1, Pallas kernels, receive(): pl.pallas_call(receive_kernel, out_shape=(jax.ShapeDtypeStruct((rows, len...  19.9 us
    all_to_all x1, blocking collectives, local(): lax.all_to_all(parts, 'tm', 0, 0, tiled=True)  17.1 us
    all_to_all x1, blocking collectives, local(): solved = lax.all_to_all(mine, 'tm', 0, 0, tiled=True)  11 us
    pallas_call x1, Pallas kernels, cancel(): pl.pallas_call(cancel_kernel, out_shape=(jax.ShapeDtypeStruct((rows, leng...  7.49 us
    ppermute x2, starting transfers between devices, passed_along(): lax.ppermute(array, axis, [(i, (i + by) % peers) for i in range(peers)])  7.22 us
    all_to_all x1, waiting for transfers between devices, local(): corr = lax.all_to_all(my_corr, 'tm', 0, 0, tiled=True).reshape(256, LANES)  6.9 us
    all_to_all x1, starting transfers between devices, local(): corr = lax.all_to_all(my_corr, 'tm', 0, 0, tiled=True).reshape(256, LANES)  3.96 us
  transfers between devices with their start and end apart: 4, of which 2 were waited for; matrix products, arithmetic and copies ran while one was open for 2% of the time, Pallas kernels for 0%

profile of v3, /device:TPU:1, one launch (start us, length us, event | category | flops | bytes accessed | tf_op | source)
XLA Modules:
  0.0 125.2 jit_solution(8533400435773502123)
XLA Ops:
  0.8 1.2 fusion.8
  2.6 0.5 fusion.15
  3.7 0.5 fusion.2
  4.3 0.6 fusion.26
  4.9 0.6 fusion.30
  5.5 0.6 fusion
  6.5 0.6 fusion.1
  7.6 6.5 %collective-permute-start.2 = (bf16[16,8192]{1,0:T(8,128)(2,1)S(1)}, bf16[16,8192]{1,0:T(8,128)(2,1)S(1)}, u32[]{:S(2)}, u32[]{:S(2)}) collective-permute-start(bf16[16,8192]{1,0:T(8,128)(2,1)S(1)} %maximum_bitcast_fusion), channel_id=1, source_target_pairs={{0,224},{32,0},{64,32},{96,64},{128,96},{160,128},{192,160},{224,1... | collective-permute-start | bytes 786440 | tf_op jit(solution)/shard_map/ppermute | solution.py:29
  14.1 3.9 %collective-permute-start = (bf16[16,128]{1,0:T(8,128)(2,1)S(1)}, bf16[16,128]{1,0:T(8,128)(2,1)S(1)}, u32[]{:S(2)}, u32[]{:S(2)}) collective-permute-start(bf16[16,128]{1,0:T(8,128)(2,1)S(1)} %slice.23), channel_id=1, source_target_pairs={{0,1},{1,2},{2,3},{3,4},{4,5},{5,6},{6,7},{7,8},{8,9},{9,10},{10,1... | collective-permute-start | bytes 12296 | tf_op jit(solution)/shard_map/ppermute | solution.py:35
  18.4 0.6 fusion.68.slot_ref
  19.4 0.8 collective-permute-start.1
  20.9 0.8 copy-done
  21.9 0.8 maximum_maximum_fusion.refs_ref
  22.8 19.9 %receive.1 = (bf16[64,8192]{1,0:T(8,128)(2,1)}, f32[32,1792]{1,0:T(8,128)}, bf16[512,8320]{1,0:T(8,128)(2,1)}) custom-call(s32[32,6]{1,0:T(8,128)} %fusion.68.slot_ref, bf16[512,512]{1,0:T(8,128)(2,1)} %copy-done, bf16[32,8320]{1,0:T(8,128)(2,1)} %maximum_maximum_fusion.refs_ref, bf16[64,8192]{1,0:T(8,128)(2,1)} %bitcast.58), custom_call_target="tpu_custom_call" | custom-call | tf_op jit(solution)/shard_map/receive/pallas_call | solution.py:348
  42.7 1.2 copy.41
  43.9 17.1 %all_to_all.26 = f32[32,1,1792]{2,1,0:T(1,128)S(1)} all-to-all(f32[32,1,1792]{2,1,0:T(1,128)S(1)} %copy.41), channel_id=1, replica_groups=mesh['chan'=8,'tm'=32] {'tm'}, dimensions={0} | all-to-all | bytes 458752 | tf_op jit(solution)/shard_map/all_to_all | solution.py:614
  61.1 0.7 broadcast_in_dim.67
  61.9 4.0 %all-to-all-start.1 = ((f32[32,1,1024]{2,1,0:T(1,128)}), f32[32,1,1024]{2,1,0:T(1,128)S(1)}, u32[]{:S(2)}, u32[]{:S(2)}) async-start(f32[32,1,1024]{2,1,0:T(1,128)} %broadcast_in_dim.67), calls=%async_computation.1 | async-start | bytes 262144 | tf_op jit(solution)/shard_map/all_to_all | solution.py:617
  65.8 0.7 dynamic-slice_bitcast_fusion.slot_ref
  66.5 6.9 %all-to-all-done.1 = f32[32,1,1024]{2,1,0:T(1,128)S(1)} async-done(((f32[32,1,1024]{2,1,0:T(1,128)}), f32[32,1,1024]{2,1,0:T(1,128)S(1)}, u32[]{:S(2)}, u32[]{:S(2)}) %all-to-all-start.1) | async-done | bytes 131104 | tf_op jit(solution)/shard_map/all_to_all | solution.py:617
  73.4 32.3 %solve.1 = f32[32,768]{1,0:T(8,128)S(1)} custom-call(s32[6]{0:T(128)S(1)} %dynamic-slice_bitcast_fusion.slot_ref, f32[256,128]{1,0:T(8,128)S(1)} %bitcast.56, f32[1,768]{1,0:T(1,128)S(1)} %slice.25.cross_ref), custom_call_target="tpu_custom_call" | custom-call | tf_op jit(solution)/shard_map/solve/pallas_call | solution.py:561
  105.9 11.0 %all_to_all.27 = f32[32,1,768]{2,1,0:T(1,128)S(1)} all-to-all(f32[32,1,768]{2,1,0:T(1,128)S(1)} %copy.42), channel_id=1, replica_groups=mesh['chan'=8,'tm'=32] {'tm'}, dimensions={0} | all-to-all | bytes 196608 | tf_op jit(solution)/shard_map/all_to_all | solution.py:620
  116.9 0.6 copy.57
  117.6 7.5 %cancel.1 = (bf16[64,8192]{1,0:T(8,128)(2,1)}, f32[2,32,384]{2,1,0:T(8,128)}) custom-call(f32[32,768]{1,0:T(8,128)} %bitcast.59, s32[192,128]{1,0:T(8,128)} %copy-done.1, bf16[512,8320]{1,0:T(8,128)(2,1)} %get-tuple-element.8.kept_ref, bf16[64,8192]{1,0:T(8,128)(2,1)} %get-tuple-element.9.received_ref), custom_call_target="tpu_custom_call" | custom-call | tf_op jit(solution)/shard_map/cancel/pallas_call | solution.py:409
  (44 shorter events, 3.9 us)
Async XLA Ops:
  7.3 10.7 %copy-start.4 = (s32[32,6]{0,1:T(8,128)S(1)}, s32[32,6]{0,1:T(8,128)}, u32[]{:S(2)}) copy-start(s32[32,6]{0,1:T(8,128)} %param.7) | copy-start | bytes 2308
  7.4 10.8 %copy-start.2 = (f32[2,32,6]{1,0,2:T(2,128)S(1)}, f32[2,32,6]{1,0,2:T(2,128)}, u32[]{:S(2)}) copy-start(f32[2,32,6]{1,0,2:T(2,128)} %param.8) | copy-start | bytes 4612
  7.4 11.0 %copy-start.3 = (s32[32,6]{0,1:T(8,128)S(1)}, s32[32,6]{0,1:T(8,128)}, u32[]{:S(2)}) copy-start(s32[32,6]{0,1:T(8,128)} %param.6) | copy-start | bytes 2308
  7.6 14.3 %collective-permute-start.2 = (bf16[16,8192]{1,0:T(8,128)(2,1)S(1)}, bf16[16,8192]{1,0:T(8,128)(2,1)S(1)}, u32[]{:S(2)}, u32[]{:S(2)}) collective-permute-start(bf16[16,8192]{1,0:T(8,128)(2,1)S(1)} %maximum_bitcast_fusion), channel_id=1, source_target_pairs={{0,224},{32,0},{64,32},{96,64},{128,96},{160,128},{192,160},{224,1... | collective-permute-start | bytes 786440 | tf_op jit(solution)/shard_map/ppermute | solution.py:29
  14.1 5.3 %collective-permute-start = (bf16[16,128]{1,0:T(8,128)(2,1)S(1)}, bf16[16,128]{1,0:T(8,128)(2,1)S(1)}, u32[]{:S(2)}, u32[]{:S(2)}) collective-permute-start(bf16[16,128]{1,0:T(8,128)(2,1)S(1)} %slice.23), channel_id=1, source_target_pairs={{0,1},{1,2},{2,3},{3,4},{4,5},{5,6},{6,7},{7,8},{8,9},{9,10},{10,1... | collective-permute-start | bytes 12296 | tf_op jit(solution)/shard_map/ppermute | solution.py:35
  19.4 2.5 %collective-permute-start.1 = (bf16[16,128]{1,0:T(8,128)(2,1)S(1)}, bf16[16,128]{1,0:T(8,128)(2,1)S(1)}, u32[]{:S(2)}, u32[]{:S(2)}) collective-permute-start(bf16[16,128]{1,0:T(8,128)(2,1)S(1)} %collective-permute-done), channel_id=1, source_target_pairs={{0,224},{32,0},{64,32},{96,64},{128,96},{160,128},{192,160},{224,1... | collective-permute-start | bytes 12296 | tf_op jit(solution)/shard_map/ppermute | solution.py:29
  20.3 0.6 copy-start.1
  20.9 0.8 copy-start
  61.9 11.6 %all-to-all-start.1 = ((f32[32,1,1024]{2,1,0:T(1,128)}), f32[32,1,1024]{2,1,0:T(1,128)S(1)}, u32[]{:S(2)}, u32[]{:S(2)}) async-start(f32[32,1,1024]{2,1,0:T(1,128)} %broadcast_in_dim.67), calls=%async_computation.1 | async-start | bytes 262144 | tf_op jit(solution)/shard_map/all_to_all | solution.py:617

commit v4 on v3

--- a/solution.py
+++ b/solution.py
@@ -2,6 +2,7 @@
 
 import jax
 import jax.numpy as jnp
+import numpy as np
 from jax import lax
 from jax.experimental import pallas as pl
 from jax.experimental.pallas import tpu as pltpu
@@ -35,66 +36,112 @@
     return lax.ppermute(block, axis, route)
 
 
-def rotation_angle_grid(row_count, col_count, period):
-    product = (
-        jnp.arange(row_count, dtype=jnp.int32)[:, None]
-        * jnp.arange(col_count, dtype=jnp.int32)[None, :]
-    )
-    phases = (product % period).astype(jnp.float32) * (2.0 * math.pi / period)
-    return (jnp.cos(phases), jnp.sin(phases))
-
-
-def complex_multiply_result(pattern, left_pair, right_pair):
-    real_part = jnp.einsum(pattern, left_pair[0], right_pair[0], precision=HIGHEST) - jnp.einsum(
-        pattern, left_pair[1], right_pair[1], precision=HIGHEST
-    )
-    imag_part = jnp.einsum(pattern, left_pair[0], right_pair[1], precision=HIGHEST) + jnp.einsum(
-        pattern, left_pair[1], right_pair[0], precision=HIGHEST
-    )
-    return (real_part, imag_part)
+def parts_of(table, count):
+    parts = []
+    for _ in range(count):
+        part = table.astype(jnp.bfloat16)
+        parts.append(part)
+        table = table - part.astype(np.float64)
+    return parts
+
+
+def wave_tables(length):
+    tiles = length // LANES
+    turn = 2.0 * np.pi / tiles
+
+    def real_form(angle):
+        return np.block([[np.cos(angle), -np.sin(angle)], [np.sin(angle), np.cos(angle)]])
+
+    q = np.arange(tiles)
+    v = np.arange(LANES)
+    first = real_form(turn * ((q[:, None] * q[None, :]) % tiles))
+    second = real_form(turn * ((q[:, None] * v[None, :]) % tiles))
+    angle = 2.0 * np.pi / length * (v[:, None] * v[None, :])
+    size = (1 - 2 * (v % 2))[:, None] / math.sqrt(ACTIVE * 42.0)
+    between = np.stack([np.cos(angle) * size, np.sin(angle) * size]).astype(np.float32)
+    high, low = parts_of(second, 2)
+    return (
+        np.concatenate(parts_of(first, 3), axis=1),
+        np.concatenate([low, high, high], axis=1),
+        between,
+    )
+
+
+def remodulate_kernel(symbols_ref, first_ref, second_ref, between_ref, out_ref, points, samples):
+    emitters, length = symbols_ref.shape
+    tiles = length // LANES
+    for q in range(tiles):
+        cols = slice(q * LANES, (q + 1) * LANES)
+        symbol = symbols_ref[:, cols].astype(jnp.float32)
+        column = jnp.floor(symbol * 0.125)
+        tone = iota((1, LANES), 1) + (q * LANES - length // 2)
+        used = (tone <= (ACTIVE - 1) // 2) & (tone >= -((ACTIVE - 1) // 2))
+        rows = slice(q * emitters, (q + 1) * emitters)
+        points[0, rows, :] = jnp.where(used, 2.0 * (symbol - 8.0 * column) - 7.0, 0.0)
+        points[1, rows, :] = jnp.where(used, 2.0 * column - 7.0, 0.0)
+    every = [pl.ds(n, tiles, stride=emitters) for n in range(emitters)]
+    grid = jnp.concatenate(
+        [
+            jnp.concatenate([points[part, rows, :] for rows in every], axis=1).astype(jnp.bfloat16)
+            for part in range(2)
+        ],
+        axis=0,
+    )
+    partial = jnp.dot(
+        first_ref[...], jnp.concatenate([grid] * 3, axis=0), preferred_element_type=jnp.float32
+    )
+    turned = []
+    for n in range(emitters):
+        cols = slice(n * LANES, (n + 1) * LANES)
+        real = jnp.concatenate([partial[:tiles, cols]] * 2, axis=0)
+        imag = jnp.concatenate([partial[tiles:, cols]] * 2, axis=0)
+        turned.append(
+            jnp.concatenate(
+                [
+                    real * between_ref[0] - imag * between_ref[1],
+                    real * between_ref[1] + imag * between_ref[0],
+                ],
+                axis=1,
+            )
+        )
+    turned = jnp.concatenate(turned, axis=0)
+    high = turned.astype(jnp.bfloat16)
+    low = (turned - high.astype(jnp.float32)).astype(jnp.bfloat16)
+    wave = lax.dot_general(
+        second_ref[...],
+        jnp.concatenate([high, low, high], axis=1),
+        (((1,), (1,)), ((), ())),
+        preferred_element_type=jnp.float32,
+    )
+    for part in range(2):
+        for n in range(emitters):
+            samples[part, every[n], :] = wave[
+                part * tiles : (part + 1) * tiles, n * LANES : (n + 1) * LANES
+            ]
+    for q in range(tiles):
+        rows = slice(q * emitters, (q + 1) * emitters)
+        out_ref[:, q * LANES : (q + 1) * LANES] = jnp.concatenate(
+            [samples[0, rows, :], samples[1, rows, :]], axis=0
+        ).astype(jnp.bfloat16)
 
 
 def remodulate(symbols):
-    emitter_number, length = symbols.shape
-    column_entries = 128
-    increment_spacing = length // column_entries
-    inphase_amplitude = (2 * (symbols % 8) - 7).astype(jnp.float32) / math.sqrt(42.0)
-    quadrature_amplitude = (2 * (symbols // 8) - 7).astype(jnp.float32) / math.sqrt(42.0)
-    subcarrier = jnp.arange(length, dtype=jnp.int32) - length // 2
-    occupied_tones = (jnp.abs(subcarrier) <= (ACTIVE - 1) // 2).astype(jnp.float32)
-    tone_symbols = (
-        (inphase_amplitude * occupied_tones).reshape(
-            emitter_number, increment_spacing, column_entries
-        ),
-        (quadrature_amplitude * occupied_tones).reshape(
-            emitter_number, increment_spacing, column_entries
-        ),
-    )
-    partial_result = complex_multiply_result(
-        "mb,nbd->nmd",
-        rotation_angle_grid(increment_spacing, increment_spacing, increment_spacing),
-        tone_symbols,
-    )
-    twiddle = rotation_angle_grid(increment_spacing, column_entries, length)
-    partial_result = (
-        partial_result[0] * twiddle[0] - partial_result[1] * twiddle[1],
-        partial_result[0] * twiddle[1] + partial_result[1] * twiddle[0],
-    )
-    frequency_spectrum = complex_multiply_result(
-        "pho,oj->phj",
-        partial_result,
-        rotation_angle_grid(column_entries, column_entries, column_entries),
-    )
-    alternate = (1 - 2 * (jnp.arange(length, dtype=jnp.int32) % 2)).astype(jnp.float32) / math.sqrt(
-        ACTIVE
-    )
-    real_part = (
-        jnp.swapaxes(frequency_spectrum[0], 1, 2).reshape(emitter_number, length) * alternate
-    )
-    imag_part = (
-        jnp.swapaxes(frequency_spectrum[1], 1, 2).reshape(emitter_number, length) * alternate
-    )
-    return jnp.stack([real_part, imag_part], axis=0).astype(jnp.bfloat16)
+    emitters, length = symbols.shape
+    vmem = pl.BlockSpec(memory_space=pltpu.VMEM)
+    first, second, between = (jnp.asarray(table) for table in wave_tables(length))
+    return pl.pallas_call(
+        remodulate_kernel,
+        out_shape=jax.ShapeDtypeStruct((2 * emitters, length), jnp.bfloat16),
+        in_specs=[vmem] * 4,
+        out_specs=vmem,
+        scratch_shapes=[
+            pltpu.VMEM((2, emitters * length // LANES, LANES), jnp.float32),
+            pltpu.VMEM((2, emitters * length // LANES, LANES), jnp.float32),
+        ],
+        compiler_params=pltpu.CompilerParams(vmem_limit_bytes=24 * 2**20),
+        cost_estimate=pl.CostEstimate(flops=2 * 10**9, bytes_accessed=10**6, transcendentals=0),
+        name="remodulate",
+    )(symbols, first, second, between)
 
 
 def iota(shape, axis):
@@ -482,6 +529,23 @@
     return jnp.dot(left, right, precision=HIGHEST, preferred_element_type=jnp.float32)
 
 
+def three_parts(array):
+    high = array.astype(jnp.bfloat16)
+    rest = array - high.astype(jnp.float32)
+    middle = rest.astype(jnp.bfloat16)
+    return high, middle, (rest - middle.astype(jnp.float32)).astype(jnp.bfloat16)
+
+
+def deep_dot(left, right):
+    lh, lm, ll = three_parts(left)
+    rh, rm, rl = three_parts(right)
+    return jnp.dot(
+        jnp.concatenate([ll, lh, lm, lm, lh, lh], axis=1),
+        jnp.concatenate([rh, rl, rm, rh, rm, rh], axis=0),
+        preferred_element_type=jnp.float32,
+    )
+
+
 def solve_kernel(slot_ref, corr_ref, cross_ref, out_ref, system, pairs):
     count = PER_RECV
     size = DELAYS
@@ -524,11 +588,11 @@
         over = inverse(system[mine, col])
         system[mine, col] = unit
         right = system[mine, :]
-        scaled = exact_dot(over, jnp.concatenate([right, times_i(right)], axis=0))
+        scaled = deep_dot(over, jnp.concatenate([right, times_i(right)], axis=0))
         factors = system[:, col]
         system[:, col] = jnp.zeros((count * size, LANES), jnp.float32)
         both = jnp.concatenate([scaled, times_i(scaled)], axis=0)
-        system[...] = system[...] - exact_dot(factors, both)
+        system[...] = system[...] - deep_dot(factors, both)
         system[mine, :] = scaled
         return 0
 
@@ -579,10 +643,12 @@
     tm_count = lax.axis_size("tm")
     tm_index = lax.axis_index("tm")
     recv_count = echoes.shape[1]
-    own = remodulate(symbols).reshape(2 * owned, length)
-    following = passed_along(own, "chan", -1)
+    sent = symbols.astype(jnp.bfloat16)
+    next_symbols = passed_along(sent, "chan", -1)
+    own = remodulate(sent)
     own_halo = from_behind(own[:, length - LANES :], "tm", 1)
     next_halo = passed_along(own_halo, "chan", -1)
+    following = remodulate(next_symbols)
     refs = jnp.concatenate(
         [
             jnp.concatenate([own_halo, own], axis=1),

time: 126 us -> 119 us (0.944)
  matrix products: 4.62 us -> 0 us
  local copies, waits for them, and re-layouts: 5.72 us -> 7.66 us
  Pallas kernels: 60.2 us -> 58.5 us
  blocking collectives: 28.1 us -> 26.6 us
    dot_general x8 -> x0, matrix products: 4.62 us -> none  [the longest x2 1.16 us: complex_multiply_result(): jnp.einsum(pattern, left_pair[1], right_pair[0], precision=HIGHEST)]
    pallas_call x1, Pallas kernels: 32.3 us -> 28.5 us  [solve(): pl.pallas_call(solve_kernel, out_shape=jax.ShapeDtypeStruct((peers, PER_R...]
    unnamed x12 -> x24, local copies, waits for them, and re-layouts: 1.75 us -> 4.46 us
    pallas_call x0 -> x2, Pallas kernels: none -> 2.18 us  [remodulate(): pl.pallas_call(remodulate_kernel, out_shape=jax.ShapeDtypeStruct((2 * emi...]
    all_to_all x1, blocking collectives: 17.1 us -> 15.6 us  [local(): lax.all_to_all(parts, 'tm', 0, 0, tiled=True)]
  transfers between devices with their start and end apart: 4 -> 4, of which waited for: 2 -> 2; matrix products, arithmetic and copies ran while one was open for 2% -> 2% of each run, Pallas kernels for 0% -> 2%
where the time goes in v4:
time: 119 us
  Pallas kernels  58.5 us (49%)
  blocking collectives  26.6 us (22%)
  starting transfers between devices  15 us (13%)
  local copies, waits for them, and re-layouts  7.66 us (6%)
  waiting for transfers between devices  7.46 us (6%)
  other arithmetic  2.78 us (2%)
    pallas_call x1, Pallas kernels, solve(): pl.pallas_call(solve_kernel, out_shape=jax.ShapeDtypeStruct((peers, PER_R...  28.5 us
    pallas_call x1, Pallas kernels, receive(): pl.pallas_call(receive_kernel, out_shape=(jax.ShapeDtypeStruct((rows, len...  20 us
    all_to_all x1, blocking collectives, local(): lax.all_to_all(parts, 'tm', 0, 0, tiled=True)  15.6 us
    all_to_all x1, blocking collectives, local(): solved = lax.all_to_all(mine, 'tm', 0, 0, tiled=True)  11 us
    pallas_call x1, Pallas kernels, cancel(): pl.pallas_call(cancel_kernel, out_shape=(jax.ShapeDtypeStruct((rows, leng...  7.49 us
    ppermute x2, starting transfers between devices, passed_along(): lax.ppermute(array, axis, [(i, (i + by) % peers) for i in range(peers)])  7.2 us
    all_to_all x1, waiting for transfers between devices, local(): corr = lax.all_to_all(my_corr, 'tm', 0, 0, tiled=True).reshape(256, LANES)  6.85 us
    unnamed x24, local copies, waits for them, and re-layouts  4.46 us
  transfers between devices with their start and end apart: 4, of which 2 were waited for; matrix products, arithmetic and copies ran while one was open for 2% of the time, Pallas kernels for 2%

profile of v4, /device:TPU:1, one launch (start us, length us, event | category | flops | bytes accessed | tf_op | source)
XLA Modules:
  0.0 119.0 jit_solution(2878152864450401957)
XLA Ops:
  0.6 1.0 convert_element_type.11.symbols_ref
  1.6 6.5 %collective-permute-start.2 = (bf16[8,8192]{1,0:T(8,128)(2,1)S(1)}, bf16[8,8192]{1,0:T(8,128)(2,1)S(1)}, u32[]{:S(2)}, u32[]{:S(2)}) collective-permute-start(bf16[8,8192]{1,0:T(8,128)(2,1)S(1)} %convert_element_type.11.symbols_ref), channel_id=1, source_target_pairs={{0,224},{32,0},{64,32},{96,64},{128,96},{160,128},{192,160},{224,1... | collective-permute-start | bytes 393224 | tf_op jit(solution)/shard_map/ppermute | solution.py:30
  8.1 0.9 copy-done.2
  9.0 0.9 copy-done.4
  9.9 0.9 copy-done.6
  10.8 1.1 remodulate.2
  11.9 4.0 %collective-permute-start = (bf16[16,128]{1,0:T(8,128)(2,1)S(1)}, bf16[16,128]{1,0:T(8,128)(2,1)S(1)}, u32[]{:S(2)}, u32[]{:S(2)}) collective-permute-start(bf16[16,128]{1,0:T(8,128)(2,1)S(1)} %slice.23), channel_id=1, source_target_pairs={{0,1},{1,2},{2,3},{3,4},{4,5},{5,6},{6,7},{7,8},{8,9},{9,10},{10,1... | collective-permute-start | bytes 12296 | tf_op jit(solution)/shard_map/ppermute | solution.py:36
  16.0 0.6 fusion.4.slot_ref
  18.0 0.8 copy-done
  18.8 0.7 collective-permute-start.1
  19.6 1.1 remodulate.3
  20.7 0.6 collective-permute-done.1
  21.3 0.8 maximum_maximum_fusion.refs_ref
  22.1 20.0 %receive.1 = (bf16[64,8192]{1,0:T(8,128)(2,1)}, f32[32,1792]{1,0:T(8,128)}, bf16[512,8320]{1,0:T(8,128)(2,1)}) custom-call(s32[32,6]{1,0:T(8,128)} %fusion.4.slot_ref, bf16[512,512]{1,0:T(8,128)(2,1)} %copy-done, bf16[32,8320]{1,0:T(8,128)(2,1)} %maximum_maximum_fusion.refs_ref, bf16[64,8192]{1,0:T(8,128)(2,1)} %bitcast.24), custom_call_target="tpu_custom_call" | custom-call | tf_op jit(solution)/shard_map/receive/pallas_call | solution.py:395
  42.1 1.2 copy.31
  43.2 15.6 %all_to_all.26 = f32[32,1,1792]{2,1,0:T(1,128)S(1)} all-to-all(f32[32,1,1792]{2,1,0:T(1,128)S(1)} %copy.31), channel_id=1, replica_groups=mesh['chan'=8,'tm'=32] {'tm'}, dimensions={0} | all-to-all | bytes 458752 | tf_op jit(solution)/shard_map/all_to_all | solution.py:680
  59.0 0.7 broadcast_in_dim.53
  59.7 3.8 %all-to-all-start.1 = ((f32[32,1,1024]{2,1,0:T(1,128)}), f32[32,1,1024]{2,1,0:T(1,128)S(1)}, u32[]{:S(2)}, u32[]{:S(2)}) async-start(f32[32,1,1024]{2,1,0:T(1,128)} %broadcast_in_dim.53), calls=%async_computation.1 | async-start | bytes 262144 | tf_op jit(solution)/shard_map/all_to_all | solution.py:683
  63.5 0.7 dynamic-slice_bitcast_fusion.slot_ref
  64.2 6.9 %all-to-all-done.1 = f32[32,1,1024]{2,1,0:T(1,128)S(1)} async-done(((f32[32,1,1024]{2,1,0:T(1,128)}), f32[32,1,1024]{2,1,0:T(1,128)S(1)}, u32[]{:S(2)}, u32[]{:S(2)}) %all-to-all-start.1) | async-done | bytes 131104 | tf_op jit(solution)/shard_map/all_to_all | solution.py:683
  71.1 28.5 %solve.1 = f32[32,768]{1,0:T(8,128)S(1)} custom-call(s32[6]{0:T(128)S(1)} %dynamic-slice_bitcast_fusion.slot_ref, f32[256,128]{1,0:T(8,128)S(1)} %bitcast.22, f32[1,768]{1,0:T(1,128)S(1)} %slice.25.cross_ref), custom_call_target="tpu_custom_call" | custom-call | tf_op jit(solution)/shard_map/solve/pallas_call | solution.py:625
  99.7 11.0 %all_to_all.27 = f32[32,1,768]{2,1,0:T(1,128)S(1)} all-to-all(f32[32,1,768]{2,1,0:T(1,128)S(1)} %copy.32), channel_id=1, replica_groups=mesh['chan'=8,'tm'=32] {'tm'}, dimensions={0} | all-to-all | bytes 196608 | tf_op jit(solution)/shard_map/all_to_all | solution.py:686
  110.7 0.6 copy.39
  111.4 7.5 %cancel.1 = (bf16[64,8192]{1,0:T(8,128)(2,1)}, f32[2,32,384]{2,1,0:T(8,128)}) custom-call(f32[32,768]{1,0:T(8,128)} %bitcast.25, s32[192,128]{1,0:T(8,128)} %copy-done.1, bf16[512,8320]{1,0:T(8,128)(2,1)} %get-tuple-element.8.kept_ref, bf16[64,8192]{1,0:T(8,128)(2,1)} %get-tuple-element.9.received_ref), custom_call_target="tpu_custom_call" | custom-call | tf_op jit(solution)/shard_map/cancel/pallas_call | solution.py:456
  (41 shorter events, 1.7 us)
Async XLA Ops:
  1.6 18.0 %collective-permute-start.2 = (bf16[8,8192]{1,0:T(8,128)(2,1)S(1)}, bf16[8,8192]{1,0:T(8,128)(2,1)S(1)}, u32[]{:S(2)}, u32[]{:S(2)}) collective-permute-start(bf16[8,8192]{1,0:T(8,128)(2,1)S(1)} %convert_element_type.11.symbols_ref), channel_id=1, source_target_pairs={{0,224},{32,0},{64,32},{96,64},{128,96},{160,128},{192,160},{224,1... | collective-permute-start | bytes 393224 | tf_op jit(solution)/shard_map/ppermute | solution.py:30
  8.1 0.9 copy-start.2
  9.0 0.9 copy-start.4
  9.9 0.9 copy-start.6
  10.8 5.1 %copy-start.9 = (s32[32,6]{0,1:T(8,128)S(1)}, s32[32,6]{0,1:T(8,128)}, u32[]{:S(2)}) copy-start(s32[32,6]{0,1:T(8,128)} %param.12) | copy-start | bytes 2308
  10.8 5.9 %copy-start.10 = (s32[32,6]{0,1:T(8,128)S(1)}, s32[32,6]{0,1:T(8,128)}, u32[]{:S(2)}) copy-start(s32[32,6]{0,1:T(8,128)} %param.13) | copy-start | bytes 2308
  10.8 6.0 %copy-start.8 = (f32[2,32,6]{1,0,2:T(2,128)S(1)}, f32[2,32,6]{1,0,2:T(2,128)}, u32[]{:S(2)}) copy-start(f32[2,32,6]{1,0,2:T(2,128)} %param.14) | copy-start | bytes 4612
  11.9 6.9 %collective-permute-start = (bf16[16,128]{1,0:T(8,128)(2,1)S(1)}, bf16[16,128]{1,0:T(8,128)(2,1)S(1)}, u32[]{:S(2)}, u32[]{:S(2)}) collective-permute-start(bf16[16,128]{1,0:T(8,128)(2,1)S(1)} %slice.23), channel_id=1, source_target_pairs={{0,1},{1,2},{2,3},{3,4},{4,5},{5,6},{6,7},{7,8},{8,9},{9,10},{10,1... | collective-permute-start | bytes 12296 | tf_op jit(solution)/shard_map/ppermute | solution.py:36
  17.4 0.6 copy-start.1
  17.4 2.2 %copy-start.3 = (bf16[128,768]{1,0:T(8,128)(2,1)S(1)}, bf16[128,768]{1,0:T(8,128)(2,1)}, u32[]{:S(2)}) copy-start(bf16[128,768]{1,0:T(8,128)(2,1)} %constant.59.clone.second_ref) | copy-start | bytes 589828
  17.4 2.2 %copy-start.5 = (f32[2,128,128]{2,1,0:T(8,128)S(1)}, f32[2,128,128]{2,1,0:T(8,128)}, u32[]{:S(2)}) copy-start(f32[2,128,128]{2,1,0:T(8,128)} %constant.60.clone.between_ref) | copy-start | bytes 393220
  17.4 2.2 %copy-start.7 = (bf16[128,384]{1,0:T(8,128)(2,1)S(1)}, bf16[128,384]{1,0:T(8,128)(2,1)}, u32[]{:S(2)}) copy-start(bf16[128,384]{1,0:T(8,128)(2,1)} %constant.58.clone.first_ref) | copy-start | bytes 294916
  18.0 0.8 copy-start
  18.8 2.5 %collective-permute-start.1 = (bf16[16,128]{1,0:T(8,128)(2,1)S(1)}, bf16[16,128]{1,0:T(8,128)(2,1)S(1)}, u32[]{:S(2)}, u32[]{:S(2)}) collective-permute-start(bf16[16,128]{1,0:T(8,128)(2,1)S(1)} %collective-permute-done), channel_id=1, source_target_pairs={{0,224},{32,0},{64,32},{96,64},{128,96},{160,128},{192,160},{224,1... | collective-permute-start | bytes 12296 | tf_op jit(solution)/shard_map/ppermute | solution.py:30
  59.7 11.4 %all-to-all-start.1 = ((f32[32,1,1024]{2,1,0:T(1,128)}), f32[32,1,1024]{2,1,0:T(1,128)S(1)}, u32[]{:S(2)}, u32[]{:S(2)}) async-start(f32[32,1,1024]{2,1,0:T(1,128)} %broadcast_in_dim.53), calls=%async_computation.1 | async-start | bytes 262144 | tf_op jit(solution)/shard_map/all_to_all | solution.py:683

commit v5 on v4

--- a/solution.py
+++ b/solution.py
@@ -39,9 +39,9 @@
 def parts_of(table, count):
     parts = []
     for _ in range(count):
-        part = table.astype(jnp.bfloat16)
+        part = table.astype(jnp.bfloat16).astype(np.float64)
         parts.append(part)
-        table = table - part.astype(np.float64)
+        table = table - part
     return parts
 
 
@@ -58,21 +58,25 @@
     second = real_form(turn * ((q[:, None] * v[None, :]) % tiles))
     angle = 2.0 * np.pi / length * (v[:, None] * v[None, :])
     size = (1 - 2 * (v % 2))[:, None] / math.sqrt(ACTIVE * 42.0)
-    between = np.stack([np.cos(angle) * size, np.sin(angle) * size]).astype(np.float32)
     high, low = parts_of(second, 2)
-    return (
-        np.concatenate(parts_of(first, 3), axis=1),
-        np.concatenate([low, high, high], axis=1),
-        between,
-    )
-
-
-def remodulate_kernel(symbols_ref, first_ref, second_ref, between_ref, out_ref, points, samples):
-    emitters, length = symbols_ref.shape
+    return np.concatenate(
+        [*parts_of(first, 3), low, high, high, np.cos(angle) * size, np.sin(angle) * size],
+        axis=1,
+        dtype=np.float32,
+    )
+
+
+def remodulate_kernel(own_ref, next_ref, table_ref, out_ref, points, samples):
+    owned, length = own_ref.shape
+    emitters = 2 * owned
+    first = table_ref[:, 0 : 3 * LANES].astype(jnp.bfloat16)
+    second = table_ref[:, 3 * LANES : 9 * LANES].astype(jnp.bfloat16)
+    along = table_ref[:, 9 * LANES : 10 * LANES]
+    across = table_ref[:, 10 * LANES :]
     tiles = length // LANES
     for q in range(tiles):
         cols = slice(q * LANES, (q + 1) * LANES)
-        symbol = symbols_ref[:, cols].astype(jnp.float32)
+        symbol = jnp.concatenate([own_ref[:, cols], next_ref[:, cols]], axis=0).astype(jnp.float32)
         column = jnp.floor(symbol * 0.125)
         tone = iota((1, LANES), 1) + (q * LANES - length // 2)
         used = (tone <= (ACTIVE - 1) // 2) & (tone >= -((ACTIVE - 1) // 2))
@@ -88,7 +92,7 @@
         axis=0,
     )
     partial = jnp.dot(
-        first_ref[...], jnp.concatenate([grid] * 3, axis=0), preferred_element_type=jnp.float32
+        first, jnp.concatenate([grid] * 3, axis=0), preferred_element_type=jnp.float32
     )
     turned = []
     for n in range(emitters):
@@ -98,8 +102,8 @@
         turned.append(
             jnp.concatenate(
                 [
-                    real * between_ref[0] - imag * between_ref[1],
-                    real * between_ref[1] + imag * between_ref[0],
+                    real * along - imag * across,
+                    real * across + imag * along,
                 ],
                 axis=1,
             )
@@ -108,7 +112,7 @@
     high = turned.astype(jnp.bfloat16)
     low = (turned - high.astype(jnp.float32)).astype(jnp.bfloat16)
     wave = lax.dot_general(
-        second_ref[...],
+        second,
         jnp.concatenate([high, low, high], axis=1),
         (((1,), (1,)), ((), ())),
         preferred_element_type=jnp.float32,
@@ -119,20 +123,24 @@
                 part * tiles : (part + 1) * tiles, n * LANES : (n + 1) * LANES
             ]
     for q in range(tiles):
-        rows = slice(q * emitters, (q + 1) * emitters)
         out_ref[:, q * LANES : (q + 1) * LANES] = jnp.concatenate(
-            [samples[0, rows, :], samples[1, rows, :]], axis=0
+            [
+                samples[part, q * emitters + side * owned : q * emitters + (side + 1) * owned, :]
+                for side in range(2)
+                for part in range(2)
+            ],
+            axis=0,
         ).astype(jnp.bfloat16)
 
 
-def remodulate(symbols):
-    emitters, length = symbols.shape
+def remodulate(own, following):
+    owned, length = own.shape
+    emitters = 2 * owned
     vmem = pl.BlockSpec(memory_space=pltpu.VMEM)
-    first, second, between = (jnp.asarray(table) for table in wave_tables(length))
     return pl.pallas_call(
         remodulate_kernel,
         out_shape=jax.ShapeDtypeStruct((2 * emitters, length), jnp.bfloat16),
-        in_specs=[vmem] * 4,
+        in_specs=[vmem] * 3,
         out_specs=vmem,
         scratch_shapes=[
             pltpu.VMEM((2, emitters * length // LANES, LANES), jnp.float32),
@@ -141,7 +149,7 @@
         compiler_params=pltpu.CompilerParams(vmem_limit_bytes=24 * 2**20),
         cost_estimate=pl.CostEstimate(flops=2 * 10**9, bytes_accessed=10**6, transcendentals=0),
         name="remodulate",
-    )(symbols, first, second, between)
+    )(own, following, jnp.asarray(wave_tables(length)))
 
 
 def iota(shape, axis):
@@ -293,9 +301,9 @@
 
 
 def receive_kernel(
-    slot_ref, taps_ref, refs_ref, echo_ref,
+    slot_ref, taps_ref, window_ref, halo_ref, echo_ref,
     received_ref, parts_ref, kept_ref,
-    shifted, signal, outer, flipped, tidy, picked, corr, sems,
+    refs_ref, shifted, signal, outer, flipped, tidy, picked, corr, sems,
 ):
     receivers = echo_ref.shape[0] // 2
     length = echo_ref.shape[1]
@@ -303,6 +311,8 @@
     heard_rows = 2 * receivers
     rows = heard_rows + 32
     groups = COARSE * heard_rows
+    refs_ref[:, 0:LANES] = halo_ref[...]
+    refs_ref[:, LANES:width] = window_ref[...]
     build_shifted(refs_ref, shifted, kept_ref, sems)
     signal[:, 0:LANES] = jnp.zeros((rows, LANES), jnp.bfloat16)
     signal[heard_rows:rows, LANES:width] = refs_ref[:, LANES:width]
@@ -385,7 +395,7 @@
     lax.fori_loop(0, width // SPAN, sent, 0)
 
 
-def receive(slot, taps, refs, echoes):
+def receive(slot, taps, refs, halo, echoes):
     rows, length = echoes.shape
     receivers = rows // 2
     width = length + LANES
@@ -399,9 +409,10 @@
             jax.ShapeDtypeStruct((receivers, PARTS), jnp.float32),
             jax.ShapeDtypeStruct((32 * FINE, width), jnp.bfloat16),
         ),
-        in_specs=[smem, vmem, vmem, vmem],
+        in_specs=[smem, vmem, vmem, vmem, vmem],
         out_specs=(vmem, vmem, pl.BlockSpec(memory_space=pl.ANY)),
         scratch_shapes=[
+            pltpu.VMEM((32, width), jnp.bfloat16),
             pltpu.VMEM((32 * FINE, width), jnp.bfloat16),
             pltpu.VMEM((rows + 32, width + LANES), jnp.bfloat16),
             pltpu.VMEM((32 * FINE, products), jnp.float32),
@@ -411,9 +422,9 @@
             pltpu.VMEM((256, LANES), jnp.float32),
             pltpu.SemaphoreType.DMA((width // SPAN,)),
         ],
-        compiler_params=pltpu.CompilerParams(vmem_limit_bytes=RECEIVE_VMEM),
+        compiler_params=pltpu.CompilerParams(vmem_limit_bytes=52 * 2**20),
         name="receive",
-    )(slot, taps, refs, echoes)
+    )(slot, taps, refs, halo, echoes)
 
 
 def cancel_kernel(
@@ -645,17 +656,8 @@
     recv_count = echoes.shape[1]
     sent = symbols.astype(jnp.bfloat16)
     next_symbols = passed_along(sent, "chan", -1)
-    own = remodulate(sent)
-    own_halo = from_behind(own[:, length - LANES :], "tm", 1)
-    next_halo = passed_along(own_halo, "chan", -1)
-    following = remodulate(next_symbols)
-    refs = jnp.concatenate(
-        [
-            jnp.concatenate([own_halo, own], axis=1),
-            jnp.concatenate([next_halo, following], axis=1),
-        ],
-        axis=0,
-    )
+    refs = remodulate(sent, next_symbols)
+    halo = from_behind(refs[:, length - LANES :], "tm", 1)
     owner_chan = incidence // owned
     slot = (owner_chan - chan_index) % chan_count * owned + incidence % owned
     slot_rows = jnp.broadcast_to(
@@ -674,7 +676,9 @@
     tap_low = (gain_taps - tap_high).astype(jnp.bfloat16)
     gain_rows = jnp.concatenate([tap_high.astype(jnp.bfloat16), tap_low], axis=0)
     laid = lay_gains(gain_rows, slot_rows)
-    received, parts, shifted = receive(slot, laid, refs, echoes.reshape(2 * recv_count, length))
+    received, parts, shifted = receive(
+        slot, laid, refs, halo, echoes.reshape(2 * recv_count, length)
+    )
     share = recv_count // tm_count
     corr_share = 256 * LANES // tm_count
     parts = jnp.sum(lax.all_to_all(parts, "tm", 0, 0, tiled=True), axis=0, keepdims=True)

time: 119 us -> 116 us (0.975)
  local copies, waits for them, and re-layouts: 7.66 us -> 5.55 us
  other arithmetic: 2.78 us -> 1.34 us
    unnamed x24 -> x6, local copies, waits for them, and re-layouts: 4.46 us -> 2.52 us
    ppermute x2 -> x1, starting transfers between devices: 7.2 us -> 6.47 us  [passed_along(): lax.ppermute(array, axis, [(i, (i + by) % peers) for i in range(peers)])]
  transfers between devices with their start and end apart: 4 -> 3, of which waited for: 2 -> 2; matrix products, arithmetic and copies ran while one was open for 2% -> 3% of each run, Pallas kernels for 2% -> 0%
where the time goes in v5:
time: 116 us
  Pallas kernels  58.2 us (50%)
  blocking collectives  27.7 us (24%)
  starting transfers between devices  14.3 us (12%)
  waiting for transfers between devices  7.77 us (7%)
  local copies, waits for them, and re-layouts  5.55 us (5%)
  other arithmetic  1.34 us (1%)
    pallas_call x1, Pallas kernels, solve(): pl.pallas_call(solve_kernel, out_shape=jax.ShapeDtypeStruct((peers, PER_R...  28.5 us
    pallas_call x1, Pallas kernels, receive(): pl.pallas_call(receive_kernel, out_shape=(jax.ShapeDtypeStruct((rows, len...  19.6 us
    all_to_all x1, blocking collectives, local(): lax.all_to_all(parts, 'tm', 0, 0, tiled=True)  16.6 us
    all_to_all x1, blocking collectives, local(): solved = lax.all_to_all(mine, 'tm', 0, 0, tiled=True)  11 us
    all_to_all x1, waiting for transfers between devices, local(): corr = lax.all_to_all(my_corr, 'tm', 0, 0, tiled=True).reshape(256, LANES)  7.52 us
    pallas_call x1, Pallas kernels, cancel(): pl.pallas_call(cancel_kernel, out_shape=(jax.ShapeDtypeStruct((rows, leng...  7.49 us
    ppermute x1, starting transfers between devices, passed_along(): lax.ppermute(array, axis, [(i, (i + by) % peers) for i in range(peers)])  6.47 us
    ppermute x1, starting transfers between devices, from_behind(): return lax.ppermute(block, axis, route)  3.96 us
  transfers between devices with their start and end apart: 3, of which 2 were waited for; matrix products, arithmetic and copies ran while one was open for 3% of the time, Pallas kernels for 0%

profile of v5, /device:TPU:1, one launch (start us, length us, event | category | flops | bytes accessed | tf_op | source)
XLA Modules:
  0.0 115.8 jit_solution(15390817314260086610)
XLA Ops:
  0.6 1.0 convert_element_type.11.own_ref
  1.6 6.5 %collective-permute-start = (bf16[8,8192]{1,0:T(8,128)(2,1)S(1)}, bf16[8,8192]{1,0:T(8,128)(2,1)S(1)}, u32[]{:S(2)}, u32[]{:S(2)}) collective-permute-start(bf16[8,8192]{1,0:T(8,128)(2,1)S(1)} %convert_element_type.11.own_ref), channel_id=1, source_target_pairs={{0,224},{32,0},{64,32},{96,64},{128,96},{160,128},{192,160},{224,1... | collective-permute-start | bytes 393224 | tf_op jit(solution)/shard_map/ppermute | solution.py:30
  8.1 0.8 eq.18
  8.8 0.8 fusion.6
  9.8 0.8 copy.19
  10.6 0.1 reduce-precision_convert_fusion
  10.8 0.1 broadcast_in_dim.50
  11.0 1.1 copy-done.1
  12.1 2.2 %remodulate.1.window_ref = bf16[32,8192]{1,0:T(8,128)(2,1)S(1)} custom-call(bf16[8,8192]{1,0:T(8,128)(2,1)S(1)} %convert_element_type.11.own_ref, bf16[8,8192]{1,0:T(8,128)(2,1)S(1)} %collective-permute-done.next_ref, f32[128,1408]{1,0:T(8,128)S(1)} %copy-done.1), custom_call_target="tpu_custom_call" | custom-call | flops 2000000000 | bytes 1000000 | tf_op jit(solution)/shard_map/remodulate/pallas_call | solution.py:140
  14.3 4.0 %collective-permute-start.1 = (bf16[32,128]{1,0:T(8,128)(2,1)S(1)}, bf16[32,128]{1,0:T(8,128)(2,1)S(1)}, u32[]{:S(2)}, u32[]{:S(2)}) collective-permute-start(bf16[32,128]{1,0:T(8,128)(2,1)S(1)} %slice.23), channel_id=1, source_target_pairs={{0,1},{1,2},{2,3},{3,4},{4,5},{5,6},{6,7},{7,8},{8,9},{9,10},{10,1... | collective-permute-start | bytes 24584 | tf_op jit(solution)/shard_map/ppermute | solution.py:36
  18.4 0.4 lay_gains.1.taps_ref
  18.8 0.2 collective-permute-done.1.halo_ref
  19.1 19.6 %receive.1 = (bf16[64,8192]{1,0:T(8,128)(2,1)}, f32[32,1792]{1,0:T(8,128)S(1)}, bf16[512,8320]{1,0:T(8,128)(2,1)}) custom-call(s32[32,6]{1,0:T(8,128)S(1)} %fusion.4.slot_ref, bf16[512,512]{1,0:T(8,128)(2,1)S(1)} %lay_gains.1.taps_ref, bf16[32,8192]{1,0:T(8,128)(2,1)S(1)} %remodulate.1.window_ref, bf16[32,128]{1,0:T(8,128)(2,1)S(1)} %collective-permute-done.1.halo_ref, ...), custom_call_target="tpu_custom_call" | custom-call | tf_op jit(solution)/shard_map/receive/pallas_call | solution.py:405
  38.7 0.2 copy.26
  38.9 16.6 %all_to_all.26 = f32[32,1,1792]{2,1,0:T(1,128)S(1)} all-to-all(f32[32,1,1792]{2,1,0:T(1,128)S(1)} %copy.26), channel_id=1, replica_groups=mesh['chan'=8,'tm'=32] {'tm'}, dimensions={0} | all-to-all | bytes 458752 | tf_op jit(solution)/shard_map/all_to_all | solution.py:684
  55.6 0.1 reduce_sum.9
  55.7 0.7 broadcast_in_dim.53
  56.5 3.8 %all-to-all-start.1 = ((f32[32,1,1024]{2,1,0:T(1,128)}), f32[32,1,1024]{2,1,0:T(1,128)S(1)}, u32[]{:S(2)}, u32[]{:S(2)}) async-start(f32[32,1,1024]{2,1,0:T(1,128)} %broadcast_in_dim.53), calls=%async_computation.1 | async-start | bytes 262144 | tf_op jit(solution)/shard_map/all_to_all | solution.py:687
  60.3 7.5 %all-to-all-done.1 = f32[32,1,1024]{2,1,0:T(1,128)S(1)} async-done(((f32[32,1,1024]{2,1,0:T(1,128)}), f32[32,1,1024]{2,1,0:T(1,128)S(1)}, u32[]{:S(2)}, u32[]{:S(2)}) %all-to-all-start.1) | async-done | bytes 131104 | tf_op jit(solution)/shard_map/all_to_all | solution.py:687
  67.8 28.5 %solve.1 = f32[32,768]{1,0:T(8,128)S(1)} custom-call(s32[6]{0:T(128)S(1)} %dynamic-slice_bitcast_fusion.slot_ref, f32[256,128]{1,0:T(8,128)S(1)} %bitcast.22, f32[1,768]{1,0:T(1,128)S(1)} %slice.25.cross_ref), custom_call_target="tpu_custom_call" | custom-call | tf_op jit(solution)/shard_map/solve/pallas_call | solution.py:636
  96.3 0.1 copy.27
  96.4 11.0 %all_to_all.27 = f32[32,1,768]{2,1,0:T(1,128)S(1)} all-to-all(f32[32,1,768]{2,1,0:T(1,128)S(1)} %copy.27), channel_id=1, replica_groups=mesh['chan'=8,'tm'=32] {'tm'}, dimensions={0} | all-to-all | bytes 196608 | tf_op jit(solution)/shard_map/all_to_all | solution.py:690
  107.5 0.6 copy.34
  108.1 7.5 %cancel.1 = (bf16[64,8192]{1,0:T(8,128)(2,1)}, f32[2,32,384]{2,1,0:T(8,128)}) custom-call(f32[32,768]{1,0:T(8,128)} %bitcast.26, s32[192,128]{1,0:T(8,128)} %copy-done, bf16[512,8320]{1,0:T(8,128)(2,1)} %get-tuple-element.8.kept_ref, bf16[64,8192]{1,0:T(8,128)(2,1)} %get-tuple-element.9.received_ref), custom_call_target="tpu_custom_call" | custom-call | tf_op jit(solution)/shard_map/cancel/pallas_call | solution.py:467
  (19 shorter events, 0.4 us)
Async XLA Ops:
  1.6 9.3 %collective-permute-start = (bf16[8,8192]{1,0:T(8,128)(2,1)S(1)}, bf16[8,8192]{1,0:T(8,128)(2,1)S(1)}, u32[]{:S(2)}, u32[]{:S(2)}) collective-permute-start(bf16[8,8192]{1,0:T(8,128)(2,1)S(1)} %convert_element_type.11.own_ref), channel_id=1, source_target_pairs={{0,224},{32,0},{64,32},{96,64},{128,96},{160,128},{192,160},{224,1... | collective-permute-start | bytes 393224 | tf_op jit(solution)/shard_map/ppermute | solution.py:30
  11.0 1.1 copy-start.1
  14.3 4.7 %collective-permute-start.1 = (bf16[32,128]{1,0:T(8,128)(2,1)S(1)}, bf16[32,128]{1,0:T(8,128)(2,1)S(1)}, u32[]{:S(2)}, u32[]{:S(2)}) collective-permute-start(bf16[32,128]{1,0:T(8,128)(2,1)S(1)} %slice.23), channel_id=1, source_target_pairs={{0,1},{1,2},{2,3},{3,4},{4,5},{5,6},{6,7},{7,8},{8,9},{9,10},{10,1... | collective-permute-start | bytes 24584 | tf_op jit(solution)/shard_map/ppermute | solution.py:36
  18.4 89.7 %copy-start = (s32[192,128]{1,0:T(8,128)}, s32[192,128]{1,0:T(8,128)S(1)}, u32[]{:S(2)}) copy-start(s32[192,128]{1,0:T(8,128)S(1)} %broadcast_in_dim.51.slot_rows_ref) | copy-start | bytes 294916
  56.5 11.4 %all-to-all-start.1 = ((f32[32,1,1024]{2,1,0:T(1,128)}), f32[32,1,1024]{2,1,0:T(1,128)S(1)}, u32[]{:S(2)}, u32[]{:S(2)}) async-start(f32[32,1,1024]{2,1,0:T(1,128)} %broadcast_in_dim.53), calls=%async_computation.1 | async-start | bytes 262144 | tf_op jit(solution)/shard_map/all_to_all | solution.py:687

commit v6 on v5

--- a/solution.py
+++ b/solution.py
@@ -17,7 +17,7 @@
 PARTS = PER_RECV * LANES + 1024
 PANEL = 4
 SPAN = 1664
-PIECE = 2048
+PIECE = 4096
 RECEIVE_VMEM = 56 * 2**20
 
 

time: 116 us -> 116 us (level)
  no operation moved by 1% of the time
where the time goes in v6:
time: 116 us; the launch traced here: 115 us
  Pallas kernels  57.6 us (50%)
  blocking collectives  27.7 us (24%)
  starting transfers between devices  14.3 us (12%)
  waiting for transfers between devices  7.77 us (7%)
  local copies, waits for them, and re-layouts  5.55 us (5%)
  other arithmetic  1.34 us (1%)
    pallas_call x1, Pallas kernels, solve(): pl.pallas_call(solve_kernel, out_shape=jax.ShapeDtypeStruct((peers, PER_R...  28.5 us
    pallas_call x1, Pallas kernels, receive(): pl.pallas_call(receive_kernel, out_shape=(jax.ShapeDtypeStruct((rows, len...  19 us
    all_to_all x1, blocking collectives, local(): lax.all_to_all(parts, 'tm', 0, 0, tiled=True)  16.6 us
    all_to_all x1, blocking collectives, local(): solved = lax.all_to_all(mine, 'tm', 0, 0, tiled=True)  11 us
    all_to_all x1, waiting for transfers between devices, local(): corr = lax.all_to_all(my_corr, 'tm', 0, 0, tiled=True).reshape(256, LANES)  7.52 us
    pallas_call x1, Pallas kernels, cancel(): pl.pallas_call(cancel_kernel, out_shape=(jax.ShapeDtypeStruct((rows, leng...  7.45 us
    ppermute x1, starting transfers between devices, passed_along(): lax.ppermute(array, axis, [(i, (i + by) % peers) for i in range(peers)])  6.47 us
    ppermute x1, starting transfers between devices, from_behind(): return lax.ppermute(block, axis, route)  3.96 us
  transfers between devices with their start and end apart: 3, of which 2 were waited for; matrix products, arithmetic and copies ran while one was open for 3% of the time, Pallas kernels for 0%

profile of v6, /device:TPU:1, one launch (start us, length us, event | category | flops | bytes accessed | tf_op | source)
XLA Modules:
  0.0 115.1 jit_solution(17896874733942132117)
XLA Ops:
  0.6 1.0 convert_element_type.11.own_ref
  1.6 6.5 %collective-permute-start = (bf16[8,8192]{1,0:T(8,128)(2,1)S(1)}, bf16[8,8192]{1,0:T(8,128)(2,1)S(1)}, u32[]{:S(2)}, u32[]{:S(2)}) collective-permute-start(bf16[8,8192]{1,0:T(8,128)(2,1)S(1)} %convert_element_type.11.own_ref), channel_id=1, source_target_pairs={{0,224},{32,0},{64,32},{96,64},{128,96},{160,128},{192,160},{224,1... | collective-permute-start | bytes 393224 | tf_op jit(solution)/shard_map/ppermute | solution.py:30
  8.1 0.8 eq.18
  8.8 0.8 fusion.6
  9.8 0.8 copy.19
  10.6 0.1 reduce-precision_convert_fusion
  10.8 0.1 broadcast_in_dim.50
  11.0 1.1 copy-done.1
  12.1 2.2 %remodulate.1.window_ref = bf16[32,8192]{1,0:T(8,128)(2,1)S(1)} custom-call(bf16[8,8192]{1,0:T(8,128)(2,1)S(1)} %convert_element_type.11.own_ref, bf16[8,8192]{1,0:T(8,128)(2,1)S(1)} %collective-permute-done.next_ref, f32[128,1408]{1,0:T(8,128)S(1)} %copy-done.1), custom_call_target="tpu_custom_call" | custom-call | flops 2000000000 | bytes 1000000 | tf_op jit(solution)/shard_map/remodulate/pallas_call | solution.py:140
  14.3 4.0 %collective-permute-start.1 = (bf16[32,128]{1,0:T(8,128)(2,1)S(1)}, bf16[32,128]{1,0:T(8,128)(2,1)S(1)}, u32[]{:S(2)}, u32[]{:S(2)}) collective-permute-start(bf16[32,128]{1,0:T(8,128)(2,1)S(1)} %slice.23), channel_id=1, source_target_pairs={{0,1},{1,2},{2,3},{3,4},{4,5},{5,6},{6,7},{7,8},{8,9},{9,10},{10,1... | collective-permute-start | bytes 24584 | tf_op jit(solution)/shard_map/ppermute | solution.py:36
  18.4 0.4 lay_gains.1.taps_ref
  18.8 0.2 collective-permute-done.1.halo_ref
  19.1 19.0 %receive.1 = (bf16[64,8192]{1,0:T(8,128)(2,1)}, f32[32,1792]{1,0:T(8,128)S(1)}, bf16[512,8320]{1,0:T(8,128)(2,1)}) custom-call(s32[32,6]{1,0:T(8,128)S(1)} %fusion.4.slot_ref, bf16[512,512]{1,0:T(8,128)(2,1)S(1)} %lay_gains.1.taps_ref, bf16[32,8192]{1,0:T(8,128)(2,1)S(1)} %remodulate.1.window_ref, bf16[32,128]{1,0:T(8,128)(2,1)S(1)} %collective-permute-done.1.halo_ref, ...), custom_call_target="tpu_custom_call" | custom-call | tf_op jit(solution)/shard_map/receive/pallas_call | solution.py:405
  38.1 0.2 copy.26
  38.4 16.6 %all_to_all.26 = f32[32,1,1792]{2,1,0:T(1,128)S(1)} all-to-all(f32[32,1,1792]{2,1,0:T(1,128)S(1)} %copy.26), channel_id=1, replica_groups=mesh['chan'=8,'tm'=32] {'tm'}, dimensions={0} | all-to-all | bytes 458752 | tf_op jit(solution)/shard_map/all_to_all | solution.py:684
  55.0 0.1 reduce_sum.9
  55.2 0.7 broadcast_in_dim.53
  55.9 3.8 %all-to-all-start.1 = ((f32[32,1,1024]{2,1,0:T(1,128)}), f32[32,1,1024]{2,1,0:T(1,128)S(1)}, u32[]{:S(2)}, u32[]{:S(2)}) async-start(f32[32,1,1024]{2,1,0:T(1,128)} %broadcast_in_dim.53), calls=%async_computation.1 | async-start | bytes 262144 | tf_op jit(solution)/shard_map/all_to_all | solution.py:687
  59.8 7.5 %all-to-all-done.1 = f32[32,1,1024]{2,1,0:T(1,128)S(1)} async-done(((f32[32,1,1024]{2,1,0:T(1,128)}), f32[32,1,1024]{2,1,0:T(1,128)S(1)}, u32[]{:S(2)}, u32[]{:S(2)}) %all-to-all-start.1) | async-done | bytes 131104 | tf_op jit(solution)/shard_map/all_to_all | solution.py:687
  67.3 28.5 %solve.1 = f32[32,768]{1,0:T(8,128)S(1)} custom-call(s32[6]{0:T(128)S(1)} %dynamic-slice_bitcast_fusion.slot_ref, f32[256,128]{1,0:T(8,128)S(1)} %bitcast.22, f32[1,768]{1,0:T(1,128)S(1)} %slice.25.cross_ref), custom_call_target="tpu_custom_call" | custom-call | tf_op jit(solution)/shard_map/solve/pallas_call | solution.py:636
  95.7 0.1 copy.27
  95.8 11.0 %all_to_all.27 = f32[32,1,768]{2,1,0:T(1,128)S(1)} all-to-all(f32[32,1,768]{2,1,0:T(1,128)S(1)} %copy.27), channel_id=1, replica_groups=mesh['chan'=8,'tm'=32] {'tm'}, dimensions={0} | all-to-all | bytes 196608 | tf_op jit(solution)/shard_map/all_to_all | solution.py:690
  106.9 0.6 copy.34
  107.5 7.5 %cancel.1 = (bf16[64,8192]{1,0:T(8,128)(2,1)}, f32[2,32,384]{2,1,0:T(8,128)}) custom-call(f32[32,768]{1,0:T(8,128)} %bitcast.26, s32[192,128]{1,0:T(8,128)} %copy-done, bf16[512,8320]{1,0:T(8,128)(2,1)} %get-tuple-element.8.kept_ref, bf16[64,8192]{1,0:T(8,128)(2,1)} %get-tuple-element.9.received_ref), custom_call_target="tpu_custom_call" | custom-call | tf_op jit(solution)/shard_map/cancel/pallas_call | solution.py:467
  (19 shorter events, 0.4 us)
Async XLA Ops:
  1.6 9.3 %collective-permute-start = (bf16[8,8192]{1,0:T(8,128)(2,1)S(1)}, bf16[8,8192]{1,0:T(8,128)(2,1)S(1)}, u32[]{:S(2)}, u32[]{:S(2)}) collective-permute-start(bf16[8,8192]{1,0:T(8,128)(2,1)S(1)} %convert_element_type.11.own_ref), channel_id=1, source_target_pairs={{0,224},{32,0},{64,32},{96,64},{128,96},{160,128},{192,160},{224,1... | collective-permute-start | bytes 393224 | tf_op jit(solution)/shard_map/ppermute | solution.py:30
  11.0 1.1 copy-start.1
  14.3 4.7 %collective-permute-start.1 = (bf16[32,128]{1,0:T(8,128)(2,1)S(1)}, bf16[32,128]{1,0:T(8,128)(2,1)S(1)}, u32[]{:S(2)}, u32[]{:S(2)}) collective-permute-start(bf16[32,128]{1,0:T(8,128)(2,1)S(1)} %slice.23), channel_id=1, source_target_pairs={{0,1},{1,2},{2,3},{3,4},{4,5},{5,6},{6,7},{7,8},{8,9},{9,10},{10,1... | collective-permute-start | bytes 24584 | tf_op jit(solution)/shard_map/ppermute | solution.py:36
  18.4 89.2 %copy-start = (s32[192,128]{1,0:T(8,128)}, s32[192,128]{1,0:T(8,128)S(1)}, u32[]{:S(2)}) copy-start(s32[192,128]{1,0:T(8,128)S(1)} %broadcast_in_dim.51.slot_rows_ref) | copy-start | bytes 294916
  55.9 11.4 %all-to-all-start.1 = ((f32[32,1,1024]{2,1,0:T(1,128)}), f32[32,1,1024]{2,1,0:T(1,128)S(1)}, u32[]{:S(2)}, u32[]{:S(2)}) async-start(f32[32,1,1024]{2,1,0:T(1,128)} %broadcast_in_dim.53), calls=%async_computation.1 | async-start | bytes 262144 | tf_op jit(solution)/shard_map/all_to_all | solution.py:687
